TPU v7x, 1024 devices: a whole 8x8x8 slice. The times are simulated.
1024 devices in a mesh: ctx: 128 (over z_lo, y, x), head: 8 (over z_hi, core).
Axes of the slice: x: 8, y: 8, z: 8 (z_hi: 4, z_lo: 2; z = z_hi * 2 + z_lo), core: 2. Of those that a mesh axis runs over, the one named last changes fastest.
Arguments:
- raw_queries: bfloat16 [16384, 4096], P('ctx', 'head'), may hold values from -4.5 to 4.5
- raw_keys: bfloat16 [16384, 4096], P('ctx', 'head'), may hold values from -4.5 to 4.5
- values: bfloat16 [16384, 4096], P('ctx', 'head'), may hold values from -6 to 6
- output_gradient: bfloat16 [16384, 4096], P('ctx', 'head'), may hold values from -16 to 16
- query_gain: float32 [4096], P('head'), may hold values from 0.1 to 1.9
- key_gain: float32 [4096], P('head'), may hold values from 0.1 to 1.9
- head_kind: int32 [32], P('head'), may hold values from 0 to 1, as said below
Outputs:
- query_gradient: bfloat16 [16384, 4096], P('ctx', 'head')
- key_gradient: bfloat16 [16384, 4096], P('ctx', 'head')
- value_gradient: bfloat16 [16384, 4096], P('ctx', 'head')
Inputs may be any that keep to these rules, and one draw needn't show every extreme that they name: `head_kind`: 1 marks a strided head and 0 a local one; each aligned group of 4 heads holds exactly one strided head.
All inputs are finite; a program needn't handle non-finite values.
Results may differ from a plain program's by a relative error of at most 0.01.
Values may be sent and summed in bfloat16 or wider, within the bound.
A program may use at most 32 MiB of HBM per device.

v0:
```python
import math

import jax
import jax.numpy as jnp
from jax import lax
from jax.sharding import PartitionSpec as P

HD = 128
WINDOW = 1024
STRIDE = 1024


EPSILON = 1e-06


def from_behind(shard, axis, by):
    count = lax.axis_size(axis)
    pairs = [(i, i + by) for i in range(count) if 0 <= i + by < count]
    return lax.ppermute(shard, axis, pairs)


def softmax_parts(scores, allowed):
    masked = jnp.where(allowed, scores, -jnp.inf)
    row_max = jnp.max(masked, axis=-1, keepdims=True)
    log_total = row_max + jnp.log(jnp.sum(jnp.exp(masked - row_max), axis=-1, keepdims=True))
    return (jnp.exp(masked - log_total), log_total)


def on_device(raw_queries, raw_keys, values, output_gradient, query_gain, key_gain, head_kind):
    row_count, local_width = raw_queries.shape
    head_count = head_kind.shape[0]
    near_count = head_count - 1
    total_width = local_width * lax.axis_size("head")
    ctx_count = lax.axis_size("ctx")
    score_scale = 1.0 / math.sqrt(HD)
    query_f = raw_queries.astype(jnp.float32)
    key_f = raw_keys.astype(jnp.float32)
    query_squares, key_squares = lax.psum(
        (jnp.sum(query_f * query_f, axis=1), jnp.sum(key_f * key_f, axis=1)), "head"
    )
    query_inverse = lax.rsqrt(query_squares / total_width + EPSILON)
    key_inverse = lax.rsqrt(key_squares / total_width + EPSILON)
    normed_queries = (query_f * query_inverse[:, None] * query_gain).astype(jnp.bfloat16)
    normed_keys = (key_f * key_inverse[:, None] * key_gain).astype(jnp.bfloat16)
    head_order = jnp.argsort(head_kind, stable=True)
    selector = (head_order[None, :] == jnp.arange(head_count, dtype=jnp.int32)[:, None]).astype(
        jnp.bfloat16
    )
    stacked = jnp.stack([normed_queries, normed_keys, values, output_gradient]).reshape(
        4, row_count, head_count, HD
    )
    sorted_heads = jnp.einsum(
        "athd,hg->atgd", stacked, selector, preferred_element_type=jnp.float32
    ).astype(jnp.bfloat16)
    near_queries = sorted_heads[0, :, :near_count]
    near_keys = sorted_heads[1, :, :near_count]
    near_values = sorted_heads[2, :, :near_count]
    near_grads = sorted_heads[3, :, :near_count]
    reach_blocks = WINDOW // row_count
    ctx_index = lax.axis_index("ctx")
    own_pair = jnp.stack([near_keys, near_values]).reshape(2, row_count, near_count * HD)
    earlier = []
    for offset in range(1, reach_blocks + 1):
        earlier.append(from_behind(own_pair, "ctx", offset))
    span_pair = jnp.concatenate(earlier[::-1] + [own_pair], axis=1).reshape(
        2, (reach_blocks + 1) * row_count, near_count, HD
    )
    span_keys = span_pair[0]
    span_values = span_pair[1]
    query_pos = ctx_index * row_count + jnp.arange(row_count, dtype=jnp.int32)
    key_pos = (ctx_index - reach_blocks) * row_count + jnp.arange(
        (reach_blocks + 1) * row_count, dtype=jnp.int32
    )
    allowed = (
        (key_pos[None, :] <= query_pos[:, None])
        & (key_pos[None, :] > query_pos[:, None] - WINDOW)
        & (key_pos[None, :] >= 0)
    )
    scores = (
        jnp.einsum("ihd,jhd->hij", near_queries, span_keys, preferred_element_type=jnp.float32)
        * score_scale
    )
    weights, log_total = softmax_parts(scores, allowed[None])
    weights_low = weights.astype(jnp.bfloat16)
    outputs = jnp.einsum(
        "hij,jhd->ihd", weights_low, span_values, preferred_element_type=jnp.float32
    )
    delta_rows = jnp.sum(near_grads.astype(jnp.float32) * outputs, axis=-1).T
    weight_grads = jnp.einsum(
        "ihd,jhd->hij", near_grads, span_values, preferred_element_type=jnp.float32
    )
    score_grads = weights * (weight_grads - delta_rows[:, :, None])
    score_low = score_grads.astype(jnp.bfloat16)
    near_query_grad = (
        jnp.einsum("hij,jhd->ihd", score_low, span_keys, preferred_element_type=jnp.float32)
        * score_scale
    ).astype(jnp.bfloat16)
    key_terms = (
        jnp.einsum("hij,ihd->jhd", score_low, near_queries, preferred_element_type=jnp.float32)
        * score_scale
    )
    value_terms = jnp.einsum(
        "hij,ihd->jhd", weights_low, near_grads, preferred_element_type=jnp.float32
    )
    block_terms = jnp.stack([key_terms, value_terms]).reshape(
        2, reach_blocks + 1, row_count, near_count * HD
    )
    own_terms = block_terms[:, reach_blocks]
    for offset in range(1, reach_blocks + 1):
        own_terms = own_terms + from_behind(block_terms[:, reach_blocks - offset], "ctx", -offset)
    near_key_grad = own_terms[0].reshape(row_count, near_count, HD).astype(jnp.bfloat16)
    near_value_grad = own_terms[1].reshape(row_count, near_count, HD).astype(jnp.bfloat16)
    per_peer = row_count // ctx_count
    period = STRIDE // row_count
    far_block = sorted_heads[:, :, near_count].reshape(4, ctx_count, per_peer, HD)
    regrouped = lax.all_to_all(far_block, "ctx", split_axis=1, concat_axis=1, tiled=True)
    far_queries = regrouped[0]
    far_keys = regrouped[1]
    far_values = regrouped[2]
    far_grads = regrouped[3]
    source = jnp.arange(ctx_count, dtype=jnp.int32)
    far_allowed = (source[None, :] <= source[:, None]) & (
        (source[:, None] - source[None, :]) % period == 0
    )
    far_scores = (
        jnp.einsum("imd,jmd->mij", far_queries, far_keys, preferred_element_type=jnp.float32)
        * score_scale
    )
    far_weights, far_total = softmax_parts(far_scores, far_allowed[None])
    far_low = far_weights.astype(jnp.bfloat16)
    far_outputs = jnp.einsum(
        "mij,jmd->imd", far_low, far_values, preferred_element_type=jnp.float32
    )
    far_delta = jnp.sum(far_grads.astype(jnp.float32) * far_outputs, axis=-1).T
    far_wgrads = jnp.einsum(
        "imd,jmd->mij", far_grads, far_values, preferred_element_type=jnp.float32
    )
    far_sgrads = (far_weights * (far_wgrads - far_delta[:, :, None])).astype(jnp.bfloat16)
    far_query_grad = (
        jnp.einsum("mij,jmd->imd", far_sgrads, far_keys, preferred_element_type=jnp.float32)
        * score_scale
    )
    far_key_grad = (
        jnp.einsum("mij,imd->jmd", far_sgrads, far_queries, preferred_element_type=jnp.float32)
        * score_scale
    )
    far_value_grad = jnp.einsum(
        "mij,imd->jmd", far_low, far_grads, preferred_element_type=jnp.float32
    )
    result = jnp.stack([far_query_grad, far_key_grad, far_value_grad]).astype(jnp.bfloat16)
    far_result = lax.all_to_all(result, "ctx", split_axis=1, concat_axis=1, tiled=True).reshape(
        3, row_count, HD
    )
    near_result = jnp.stack([near_query_grad, near_key_grad, near_value_grad])
    all_sorted = jnp.concatenate([near_result, far_result[:, :, None, :]], axis=2)
    restored = (
        jnp.einsum("atgd,hg->athd", all_sorted, selector, preferred_element_type=jnp.float32)
        .astype(jnp.bfloat16)
        .reshape(3, row_count, local_width)
    )
    return (restored[0], restored[1], restored[2])


def solution(mesh):
    placed = (
        P("ctx", "head"),
        P("ctx", "head"),
        P("ctx", "head"),
        P("ctx", "head"),
        P("head"),
        P("head"),
        P("head"),
    )
    return jax.shard_map(
        on_device,
        mesh=mesh,
        in_specs=placed,
        out_specs=(P("ctx", "head"), P("ctx", "head"), P("ctx", "head")),
        check_vma=False,
    )
```

profile of v0, /device:TPU:14, one launch (start us, length us, event | category | flops | bytes accessed | tf_op | source)
XLA Modules:
  0.0 237.8 jit_solution(2762662830172094046)
XLA Ops:
  0.6 1.0 fusion.35
  1.7 1.0 fusion.38
  2.7 28.1 %all-reduce = (f32[128]{0:T(128)S(1)}, f32[128]{0:T(128)S(1)}) all-reduce(f32[128]{0:T(128)S(1)} %fusion.38, f32[128]{0:T(128)S(1)} %fusion.35), channel_id=1, replica_groups=mesh['ctx'=128,'head'=8] {'head'}, use_global_device_ids=true, to_apply=%region_4.0 | all-reduce | flops 256 | bytes 2048 | tf_op jit(solution)/shard_map/psum | solution.py:38
  30.8 1.0 fusion.40
  31.9 1.0 fusion.37
  32.9 0.9 stack.49
  33.9 0.9 stack.50
  34.8 0.7 sort.17
  35.6 0.5 fusion.5
  36.4 3.4 %collective-permute-start.7 = (bf16[2,128,384]{1,2,0:T(8,128)(2,1)S(1)}, bf16[2,128,384]{1,2,0:T(8,128)(2,1)S(1)}, u32[]{:S(2)}, u32[]{:S(2)}) collective-permute-start(bf16[2,128,384]{1,2,0:T(8,128)(2,1)S(1)} %bitcast.168), channel_id=1, source_target_pairs={{0,8},{8,16},{16,24},{24,32},{32,40},{40,48},{48,56},{56,64},{64,7... | collective-permute-start | bytes 589832 | tf_op jit(solution)/shard_map/ppermute | solution.py:19
  39.8 4.3 %collective-permute-start.6 = (bf16[2,128,384]{1,2,0:T(8,128)(2,1)S(1)}, bf16[2,128,384]{1,2,0:T(8,128)(2,1)S(1)}, u32[]{:S(2)}, u32[]{:S(2)}) collective-permute-start(bf16[2,128,384]{1,2,0:T(8,128)(2,1)S(1)} %bitcast.169), channel_id=1, source_target_pairs={{0,16},{8,24},{16,32},{24,40},{32,48},{40,56},{48,64},{56,72},{64,... | collective-permute-start | bytes 589832 | tf_op jit(solution)/shard_map/ppermute | solution.py:19
  44.2 5.6 %collective-permute-start.5 = (bf16[2,128,384]{1,2,0:T(8,128)(2,1)S(1)}, bf16[2,128,384]{1,2,0:T(8,128)(2,1)S(1)}, u32[]{:S(2)}, u32[]{:S(2)}) collective-permute-start(bf16[2,128,384]{1,2,0:T(8,128)(2,1)S(1)} %bitcast.170), channel_id=1, source_target_pairs={{0,24},{8,32},{16,40},{24,48},{32,56},{40,64},{48,72},{56,80},{64,... | collective-permute-start | bytes 589832 | tf_op jit(solution)/shard_map/ppermute | solution.py:19
  49.7 4.5 %collective-permute-start.1 = (bf16[2,128,384]{1,2,0:T(8,128)(2,1)S(1)}, bf16[2,128,384]{1,2,0:T(8,128)(2,1)S(1)}, u32[]{:S(2)}, u32[]{:S(2)}) collective-permute-start(bf16[2,128,384]{1,2,0:T(8,128)(2,1)S(1)} %bitcast.171), channel_id=1, source_target_pairs={{0,56},{8,64},{16,72},{24,80},{32,88},{40,96},{48,104},{56,112},{6... | collective-permute-start | bytes 589832 | tf_op jit(solution)/shard_map/ppermute | solution.py:19
  54.2 3.6 %collective-permute-start = (bf16[2,128,384]{1,2,0:T(8,128)(2,1)S(1)}, bf16[2,128,384]{1,2,0:T(8,128)(2,1)S(1)}, u32[]{:S(2)}, u32[]{:S(2)}) collective-permute-start(bf16[2,128,384]{1,2,0:T(8,128)(2,1)S(1)} %bitcast.172), channel_id=1, source_target_pairs={{0,64},{8,72},{16,80},{24,88},{32,96},{40,104},{48,112},{56,120},{... | collective-permute-start | bytes 589832 | tf_op jit(solution)/shard_map/ppermute | solution.py:19
  57.8 0.3 slice.117
  58.1 0.8 copy.110
  58.9 10.7 %all-to-all-start = ((bf16[4,128,1,128]{3,0,2,1:T(4,128)(2,1)}), bf16[4,128,1,128]{3,0,2,1:T(4,128)(2,1)S(1)}, u32[]{:S(2)}, u32[]{:S(2)}) async-start(bf16[4,128,1,128]{3,0,2,1:T(4,128)(2,1)} %copy.110), calls=%async_computation | async-start | bytes 262144 | tf_op jit(solution)/shard_map/all_to_all | solution.py:116
  69.7 0.9 and_and_fusion
  70.6 0.8 copy.98
  71.6 5.2 %collective-permute-start.2 = (bf16[2,128,384]{1,2,0:T(8,128)(2,1)S(1)}, bf16[2,128,384]{1,2,0:T(8,128)(2,1)S(1)}, u32[]{:S(2)}, u32[]{:S(2)}) collective-permute-start(bf16[2,128,384]{1,2,0:T(8,128)(2,1)S(1)} %bitcast.173), channel_id=1, source_target_pairs={{0,48},{8,56},{16,64},{24,72},{32,80},{40,88},{48,96},{56,104},{64... | collective-permute-start | bytes 589832 | tf_op jit(solution)/shard_map/ppermute | solution.py:19
  76.8 4.3 %collective-permute-start.3 = (bf16[2,128,384]{1,2,0:T(8,128)(2,1)S(1)}, bf16[2,128,384]{1,2,0:T(8,128)(2,1)S(1)}, u32[]{:S(2)}, u32[]{:S(2)}) collective-permute-start(bf16[2,128,384]{1,2,0:T(8,128)(2,1)S(1)} %bitcast.174), channel_id=1, source_target_pairs={{0,40},{8,48},{16,56},{24,64},{32,72},{40,80},{48,88},{56,96},{64,... | collective-permute-start | bytes 589832 | tf_op jit(solution)/shard_map/ppermute | solution.py:19
  81.1 10.4 %collective-permute-done.2 = bf16[2,128,384]{1,2,0:T(8,128)(2,1)S(1)} collective-permute-done((bf16[2,128,384]{1,2,0:T(8,128)(2,1)S(1)}, bf16[2,128,384]{1,2,0:T(8,128)(2,1)S(1)}, u32[]{:S(2)}, u32[]{:S(2)}) %collective-permute-start.2) | collective-permute-done | bytes 196640 | tf_op jit(solution)/shard_map/ppermute | solution.py:19
  91.5 4.1 %collective-permute-start.4 = (bf16[2,128,384]{1,2,0:T(8,128)(2,1)S(1)}, bf16[2,128,384]{1,2,0:T(8,128)(2,1)S(1)}, u32[]{:S(2)}, u32[]{:S(2)}) collective-permute-start(bf16[2,128,384]{1,2,0:T(8,128)(2,1)S(1)} %bitcast.175), channel_id=1, source_target_pairs={{0,32},{8,40},{16,48},{24,56},{32,64},{40,72},{48,80},{56,88},{64,... | collective-permute-start | bytes 589832 | tf_op jit(solution)/shard_map/ppermute | solution.py:19
  95.7 2.5 %collective-permute-done.3 = bf16[2,128,384]{1,2,0:T(8,128)(2,1)S(1)} collective-permute-done((bf16[2,128,384]{1,2,0:T(8,128)(2,1)S(1)}, bf16[2,128,384]{1,2,0:T(8,128)(2,1)S(1)}, u32[]{:S(2)}, u32[]{:S(2)}) %collective-permute-start.3) | collective-permute-done | bytes 196640 | tf_op jit(solution)/shard_map/ppermute | solution.py:19
  98.2 7.9 %collective-permute-done.4 = bf16[2,128,384]{1,2,0:T(8,128)(2,1)S(1)} collective-permute-done((bf16[2,128,384]{1,2,0:T(8,128)(2,1)S(1)}, bf16[2,128,384]{1,2,0:T(8,128)(2,1)S(1)}, u32[]{:S(2)}, u32[]{:S(2)}) %collective-permute-start.4) | collective-permute-done | bytes 196640 | tf_op jit(solution)/shard_map/ppermute | solution.py:19
  106.5 0.7 copy-done.6
  107.3 0.6 fusion.63
  107.9 0.4 exponential_reduce_fusion
  108.3 1.2 fusion.43
  109.5 1.8 copy.94
  111.3 1.2 fusion.41
  112.5 2.7 %convolution_bitcast_fusion = f32[1152,3,128]{0,2,1:T(8,128)} fusion(bf16[128,3,128]{0,2,1:T(8,128)(2,1)} %copy.98, f32[3,128,1152]{2,1,0:T(8,128)S(1)} %get-tuple-element.31, f32[3,128]{1,0:T(4,128)S(1)} %log_add_fusion), kind=kOutput, calls=%fused_computation.6 | convolution fusion | flops 114130944 | bytes 3638784 | tf_op jit(solution)/shard_map/hij,ihd->jhd/dot_general | solution.py:102
  115.3 1.4 fusion.3
  116.7 2.8 %copy.99 = f32[1152,3,128]{2,1,0:T(4,128)S(1)} copy(f32[1152,3,128]{0,2,1:T(8,128)} %convolution_bitcast_fusion) | data formatting | bytes 3538944 | tf_op jit(solution)/shard_map/hij,ihd->jhd/transpose | solution.py:102
  119.5 2.3 stack.55
  121.8 2.8 %fusion.2 = f32[1152,3,128]{0,2,1:T(8,128)} fusion(bf16[128,3,128]{0,2,1:T(8,128)(2,1)S(1)} %copy.96, bf16[3,128,1152]{2,1,0:T(8,128)(2,1)} %fusion.3), kind=kOutput, calls=%fused_computation.5 | convolution fusion | flops 113688576 | bytes 2752512 | tf_op jit(solution)/shard_map/hij,ihd->jhd/dot_general | solution.py:99
  124.6 2.8 %copy.97 = f32[1152,3,128]{2,1,0:T(4,128)S(1)} copy(f32[1152,3,128]{0,2,1:T(8,128)} %fusion.2) | data formatting | bytes 3538944 | tf_op jit(solution)/shard_map/mul | solution.py:99
  127.3 2.3 stack.54
  129.6 1.7 constant_dynamic-update-slice_fusion.10
  131.4 0.3 copy-done.4
  131.8 1.6 slice_bitcast_fusion.7
  133.4 1.0 copy-done.2
  134.4 2.0 collective-permute-start.8
  136.4 1.9 collective-permute-start.13
  138.3 1.9 collective-permute-start.12
  140.3 1.9 collective-permute-start.11
  142.2 1.9 collective-permute-start.10
  145.4 31.7 %collective-permute-done.8 = f32[2,128,384]{2,1,0:T(8,128)S(1)} collective-permute-done((f32[2,128,384]{2,1,0:T(8,128)}, f32[2,128,384]{2,1,0:T(8,128)S(1)}, u32[]{:S(2)}, u32[]{:S(2)}) %collective-permute-start.8) | collective-permute-done | bytes 393248 | tf_op jit(solution)/shard_map/ppermute | solution.py:19
  177.0 1.9 collective-permute-start.9
  178.9 2.8 %collective-permute-done.13 = f32[2,128,384]{2,1,0:T(8,128)S(1)} collective-permute-done((f32[2,128,384]{2,1,0:T(8,128)}, f32[2,128,384]{2,1,0:T(8,128)S(1)}, u32[]{:S(2)}, u32[]{:S(2)}) %collective-permute-start.13) | collective-permute-done | bytes 393248 | tf_op jit(solution)/shard_map/ppermute | solution.py:19
  181.7 1.3 collective-permute-start.15
  183.0 7.0 %collective-permute-done.12 = f32[2,128,384]{2,1,0:T(8,128)} collective-permute-done((f32[2,128,384]{2,1,0:T(8,128)}, f32[2,128,384]{2,1,0:T(8,128)}, u32[]{:S(2)}, u32[]{:S(2)}) %collective-permute-start.12) | collective-permute-done | bytes 393248 | tf_op jit(solution)/shard_map/ppermute | solution.py:19
  190.0 1.9 collective-permute-start.14
  192.0 0.2 fusion.18
  192.2 0.7 copy.120
  192.9 28.7 %all-to-all-start.1 = ((bf16[3,128,1,128]{3,0,2,1:T(4,128)(2,1)}), bf16[3,128,1,128]{3,0,2,1:T(4,128)(2,1)S(1)}, u32[]{:S(2)}, u32[]{:S(2)}) async-start(bf16[3,128,1,128]{3,0,2,1:T(4,128)(2,1)} %copy.120), calls=%async_computation.1 | async-start | bytes 262144 | tf_op jit(solution)/shard_map/all_to_all | solution.py:151
  221.7 0.4 fusion.8
  222.1 10.5 %all-to-all-done.1 = bf16[3,128,1,128]{3,0,2,1:T(4,128)(2,1)S(1)} async-done(((bf16[3,128,1,128]{3,0,2,1:T(4,128)(2,1)}), bf16[3,128,1,128]{3,0,2,1:T(4,128)(2,1)S(1)}, u32[]{:S(2)}, u32[]{:S(2)}) %all-to-all-start.1) | async-done | bytes 98336 | tf_op jit(solution)/shard_map/all_to_all | solution.py:151
  232.8 1.9 fusion.34
  235.1 0.3 copy.122
  235.3 0.4 fusion.6
  235.8 0.7 copy.167
  236.5 0.7 copy.168
  237.2 0.7 copy.169
  (64 shorter events, 3.2 us)
Async XLA Ops:
  0.6 34.2 %copy-start.7 = (s32[4]{0:T(128)S(1)}, s32[4]{0:T(128)}, u32[]{:S(2)}) copy-start(s32[4]{0:T(128)} %param.13) | copy-start | bytes 52
  36.4 69.8 %collective-permute-start.7 = (bf16[2,128,384]{1,2,0:T(8,128)(2,1)S(1)}, bf16[2,128,384]{1,2,0:T(8,128)(2,1)S(1)}, u32[]{:S(2)}, u32[]{:S(2)}) collective-permute-start(bf16[2,128,384]{1,2,0:T(8,128)(2,1)S(1)} %bitcast.168), channel_id=1, source_target_pairs={{0,8},{8,16},{16,24},{24,32},{32,40},{40,48},{48,56},{56,64},{64,7... | collective-permute-start | bytes 589832 | tf_op jit(solution)/shard_map/ppermute | solution.py:19
  39.8 66.4 %collective-permute-start.6 = (bf16[2,128,384]{1,2,0:T(8,128)(2,1)S(1)}, bf16[2,128,384]{1,2,0:T(8,128)(2,1)S(1)}, u32[]{:S(2)}, u32[]{:S(2)}) collective-permute-start(bf16[2,128,384]{1,2,0:T(8,128)(2,1)S(1)} %bitcast.169), channel_id=1, source_target_pairs={{0,16},{8,24},{16,32},{24,40},{32,48},{40,56},{48,64},{56,72},{64,... | collective-permute-start | bytes 589832 | tf_op jit(solution)/shard_map/ppermute | solution.py:19
  44.2 62.0 %collective-permute-start.5 = (bf16[2,128,384]{1,2,0:T(8,128)(2,1)S(1)}, bf16[2,128,384]{1,2,0:T(8,128)(2,1)S(1)}, u32[]{:S(2)}, u32[]{:S(2)}) collective-permute-start(bf16[2,128,384]{1,2,0:T(8,128)(2,1)S(1)} %bitcast.170), channel_id=1, source_target_pairs={{0,24},{8,32},{16,40},{24,48},{32,56},{40,64},{48,72},{56,80},{64,... | collective-permute-start | bytes 589832 | tf_op jit(solution)/shard_map/ppermute | solution.py:19
  49.7 27.1 %collective-permute-start.1 = (bf16[2,128,384]{1,2,0:T(8,128)(2,1)S(1)}, bf16[2,128,384]{1,2,0:T(8,128)(2,1)S(1)}, u32[]{:S(2)}, u32[]{:S(2)}) collective-permute-start(bf16[2,128,384]{1,2,0:T(8,128)(2,1)S(1)} %bitcast.171), channel_id=1, source_target_pairs={{0,56},{8,64},{16,72},{24,80},{32,88},{40,96},{48,104},{56,112},{6... | collective-permute-start | bytes 589832 | tf_op jit(solution)/shard_map/ppermute | solution.py:19
  54.2 17.3 %collective-permute-start = (bf16[2,128,384]{1,2,0:T(8,128)(2,1)S(1)}, bf16[2,128,384]{1,2,0:T(8,128)(2,1)S(1)}, u32[]{:S(2)}, u32[]{:S(2)}) collective-permute-start(bf16[2,128,384]{1,2,0:T(8,128)(2,1)S(1)} %bitcast.172), channel_id=1, source_target_pairs={{0,64},{8,72},{16,80},{24,88},{32,96},{40,104},{48,112},{56,120},{... | collective-permute-start | bytes 589832 | tf_op jit(solution)/shard_map/ppermute | solution.py:19
  58.9 85.2 %all-to-all-start = ((bf16[4,128,1,128]{3,0,2,1:T(4,128)(2,1)}), bf16[4,128,1,128]{3,0,2,1:T(4,128)(2,1)S(1)}, u32[]{:S(2)}, u32[]{:S(2)}) async-start(bf16[4,128,1,128]{3,0,2,1:T(4,128)(2,1)} %copy.110), calls=%async_computation | async-start | bytes 262144 | tf_op jit(solution)/shard_map/all_to_all | solution.py:116
  71.6 20.0 %collective-permute-start.2 = (bf16[2,128,384]{1,2,0:T(8,128)(2,1)S(1)}, bf16[2,128,384]{1,2,0:T(8,128)(2,1)S(1)}, u32[]{:S(2)}, u32[]{:S(2)}) collective-permute-start(bf16[2,128,384]{1,2,0:T(8,128)(2,1)S(1)} %bitcast.173), channel_id=1, source_target_pairs={{0,48},{8,56},{16,64},{24,72},{32,80},{40,88},{48,96},{56,104},{64... | collective-permute-start | bytes 589832 | tf_op jit(solution)/shard_map/ppermute | solution.py:19
  76.8 21.3 %collective-permute-start.3 = (bf16[2,128,384]{1,2,0:T(8,128)(2,1)S(1)}, bf16[2,128,384]{1,2,0:T(8,128)(2,1)S(1)}, u32[]{:S(2)}, u32[]{:S(2)}) collective-permute-start(bf16[2,128,384]{1,2,0:T(8,128)(2,1)S(1)} %bitcast.174), channel_id=1, source_target_pairs={{0,40},{8,48},{16,56},{24,64},{32,72},{40,80},{48,88},{56,96},{64,... | collective-permute-start | bytes 589832 | tf_op jit(solution)/shard_map/ppermute | solution.py:19
  91.5 14.5 %collective-permute-start.4 = (bf16[2,128,384]{1,2,0:T(8,128)(2,1)S(1)}, bf16[2,128,384]{1,2,0:T(8,128)(2,1)S(1)}, u32[]{:S(2)}, u32[]{:S(2)}) collective-permute-start(bf16[2,128,384]{1,2,0:T(8,128)(2,1)S(1)} %bitcast.175), channel_id=1, source_target_pairs={{0,32},{8,40},{16,48},{24,56},{32,64},{40,72},{48,80},{56,88},{64,... | collective-permute-start | bytes 589832 | tf_op jit(solution)/shard_map/ppermute | solution.py:19
  106.4 0.9 copy-start.6
  106.5 1.8 copy-start
  112.5 2.7 %copy-start.1 = (bf16[1,1152,384]{1,2,0:T(8,128)(2,1)S(1)}, bf16[1,1152,384]{1,2,0:T(8,128)(2,1)}, u32[]{:S(2)}) copy-start(bf16[1,1152,384]{1,2,0:T(8,128)(2,1)} %copy-done) | copy-start | bytes 2654212
  112.5 2.7 %copy-start.5 = (bf16[128,3,128]{0,2,1:T(8,128)(2,1)S(1)}, bf16[128,3,128]{0,2,1:T(8,128)(2,1)}, u32[]{:S(2)}) copy-start(bf16[128,3,128]{0,2,1:T(8,128)(2,1)} %copy.98) | copy-start | bytes 294916
  129.6 2.0 copy-start.4
  131.8 2.6 %copy-start.2 = (f32[2,9,128,384]{3,2,1,0:T(8,128)}, f32[2,9,128,384]{3,2,1,0:T(8,128)S(1)}, u32[]{:S(2)}) copy-start(f32[2,9,128,384]{3,2,1,0:T(8,128)S(1)} %constant_dynamic-update-slice_fusion.9) | copy-start | bytes 10616836
  134.4 87.3 %copy-start.3 = (bf16[3,128,1152]{2,1,0:T(8,128)(2,1)S(1)}, bf16[3,128,1152]{2,1,0:T(8,128)(2,1)}, u32[]{:S(2)}) copy-start(bf16[3,128,1152]{2,1,0:T(8,128)(2,1)} %fusion.3) | copy-start | bytes 2654212
  134.4 42.7 %collective-permute-start.8 = (f32[2,128,384]{2,1,0:T(8,128)}, f32[2,128,384]{2,1,0:T(8,128)S(1)}, u32[]{:S(2)}, u32[]{:S(2)}) collective-permute-start(f32[2,128,384]{2,1,0:T(8,128)} %get-tuple-element.7), channel_id=1, source_target_pairs={{8,0},{16,8},{24,16},{32,24},{40,32},{48,40},{56,48},{64,56},{72,6... | collective-permute-start | bytes 1179656 | tf_op jit(solution)/shard_map/ppermute | solution.py:19
  136.4 45.3 %collective-permute-start.13 = (f32[2,128,384]{2,1,0:T(8,128)}, f32[2,128,384]{2,1,0:T(8,128)S(1)}, u32[]{:S(2)}, u32[]{:S(2)}) collective-permute-start(f32[2,128,384]{2,1,0:T(8,128)} %get-tuple-element.8), channel_id=1, source_target_pairs={{48,0},{56,8},{64,16},{72,24},{80,32},{88,40},{96,48},{104,56},{11... | collective-permute-start | bytes 1179656 | tf_op jit(solution)/shard_map/ppermute | solution.py:19
  138.3 51.7 %collective-permute-start.12 = (f32[2,128,384]{2,1,0:T(8,128)}, f32[2,128,384]{2,1,0:T(8,128)}, u32[]{:S(2)}, u32[]{:S(2)}) collective-permute-start(f32[2,128,384]{2,1,0:T(8,128)} %get-tuple-element.9), channel_id=1, source_target_pairs={{40,0},{48,8},{56,16},{64,24},{72,32},{80,40},{88,48},{96,56},{104... | collective-permute-start | bytes 1179656 | tf_op jit(solution)/shard_map/ppermute | solution.py:19
  140.3 92.5 %collective-permute-start.11 = (f32[2,128,384]{2,1,0:T(8,128)}, f32[2,128,384]{2,1,0:T(8,128)}, u32[]{:S(2)}, u32[]{:S(2)}) collective-permute-start(f32[2,128,384]{2,1,0:T(8,128)} %get-tuple-element.10), channel_id=1, source_target_pairs={{32,0},{40,8},{48,16},{56,24},{64,32},{72,40},{80,48},{88,56},{96,... | collective-permute-start | bytes 1179656 | tf_op jit(solution)/shard_map/ppermute | solution.py:19
  142.2 90.6 %collective-permute-start.10 = (f32[2,128,384]{2,1,0:T(8,128)}, f32[2,128,384]{2,1,0:T(8,128)}, u32[]{:S(2)}, u32[]{:S(2)}) collective-permute-start(f32[2,128,384]{2,1,0:T(8,128)} %get-tuple-element.11), channel_id=1, source_target_pairs={{24,0},{32,8},{40,16},{48,24},{56,32},{64,40},{72,48},{80,56},{88,... | collective-permute-start | bytes 1179656 | tf_op jit(solution)/shard_map/ppermute | solution.py:19
  177.0 55.8 %collective-permute-start.9 = (f32[2,128,384]{2,1,0:T(8,128)}, f32[2,128,384]{2,1,0:T(8,128)}, u32[]{:S(2)}, u32[]{:S(2)}) collective-permute-start(f32[2,128,384]{2,1,0:T(8,128)} %get-tuple-element.12), channel_id=1, source_target_pairs={{16,0},{24,8},{32,16},{40,24},{48,32},{56,40},{64,48},{72,56},{80,... | collective-permute-start | bytes 1179656 | tf_op jit(solution)/shard_map/ppermute | solution.py:19
  181.7 51.1 %collective-permute-start.15 = (f32[2,128,384]{2,1,0:T(8,128)}, f32[2,128,384]{2,1,0:T(8,128)}, u32[]{:S(2)}, u32[]{:S(2)}) collective-permute-start(f32[2,128,384]{2,1,0:T(8,128)} %get-tuple-element.13), channel_id=1, source_target_pairs={{64,0},{72,8},{80,16},{88,24},{96,32},{104,40},{112,48},{120,56},{... | collective-permute-start | bytes 1179656 | tf_op jit(solution)/shard_map/ppermute | solution.py:19
  190.0 42.8 %collective-permute-start.14 = (f32[2,128,384]{2,1,0:T(8,128)S(1)}, f32[2,128,384]{2,1,0:T(8,128)}, u32[]{:S(2)}, u32[]{:S(2)}) collective-permute-start(f32[2,128,384]{2,1,0:T(8,128)S(1)} %get-tuple-element.14), channel_id=1, source_target_pairs={{56,0},{64,8},{72,16},{80,24},{88,32},{96,40},{104,48},{112,56},{1... | collective-permute-start | bytes 1179656 | tf_op jit(solution)/shard_map/ppermute | solution.py:19
  192.9 39.7 %all-to-all-start.1 = ((bf16[3,128,1,128]{3,0,2,1:T(4,128)(2,1)}), bf16[3,128,1,128]{3,0,2,1:T(4,128)(2,1)S(1)}, u32[]{:S(2)}, u32[]{:S(2)}) async-start(bf16[3,128,1,128]{3,0,2,1:T(4,128)(2,1)} %copy.120), calls=%async_computation.1 | async-start | bytes 262144 | tf_op jit(solution)/shard_map/all_to_all | solution.py:151
where the time goes:
time: 241 us; the launch traced here: 238 us
  starting transfers between devices  89.1 us (37%)
  waiting for transfers between devices  72.8 us (30%)
  blocking collectives  28.1 us (12%)
  local copies, waits for them, and re-layouts  26.2 us (11%)
  matrix products  11.1 us (5%)
  other arithmetic  9.26 us (4%)
    ppermute x16, waiting for transfers between devices, from_behind(): return lax.ppermute(shard, axis, pairs)  62.2 us
    ppermute x16, starting transfers between devices, from_behind(): return lax.ppermute(shard, axis, pairs)  49.7 us
    all_to_all x1, starting transfers between devices, on_device(): lax.all_to_all(result, 'ctx', split_axis=1, concat_axis=1, tiled=True)  28.7 us
    psum x1, blocking collectives, on_device(): lax.psum((jnp.sum(query_f * query_f, axis=1), jnp.sum(key_f * key_f, axis...  28.1 us
    all_to_all x1, starting transfers between devices, on_device(): lax.all_to_all(far_block, 'ctx', split_axis=1, concat_axis=1, tiled=True)  10.7 us
    all_to_all x1, waiting for transfers between devices, on_device(): lax.all_to_all(result, 'ctx', split_axis=1, concat_axis=1, tiled=True)  10.5 us
    unnamed x29, local copies, waits for them, and re-layouts  6.25 us
  transfers between devices with their start and end apart: 18, of which 7 were waited for; matrix products, arithmetic and copies ran while one was open for 13% of the time, Pallas kernels for 0%

commit v1 on v0

v1 whole, which is shorter than its diff:
```python
import functools
import math

import jax
import jax.numpy as jnp
from jax import lax
from jax.experimental import pallas as pl
from jax.experimental.pallas import tpu as pltpu
from jax.sharding import PartitionSpec as P

HD = 128
WINDOW = 1024
STRIDE = 1024
EPSILON = 1e-06
NEAR = 3
MESH = pl.DeviceIdType.MESH
SCORE_SCALE = 1.0 / math.sqrt(HD)


def dot_nt(a, b):
    return lax.dot_general(a, b, (((1,), (1,)), ((), ())), preferred_element_type=jnp.float32)


def dot_tn(a, b):
    return lax.dot_general(a, b, (((0,), (0,)), ((), ())), preferred_element_type=jnp.float32)


def dot_nn(a, b):
    return lax.dot_general(a, b, (((1,), (0,)), ((), ())), preferred_element_type=jnp.float32)


def strided_index(kind_ref):
    index = kind_ref[1] + 2 * kind_ref[2] + 3 * kind_ref[3]
    return jnp.full((1, HD), index, jnp.int32)


def split_heads(heads, index):
    near = [jnp.where(index > g, heads[g], heads[g + 1]) for g in range(NEAR)]
    far = heads[NEAR]
    for g in range(NEAR):
        far = jnp.where(index == g, heads[g], far)
    return near, far


def join_heads(near, far, index):
    joined = []
    for h in range(NEAR + 1):
        if h == 0:
            kept = near[0]
            joined.append(jnp.where(index == 0, far, kept))
        elif h == NEAR:
            joined.append(jnp.where(index == h, far, near[h - 1]))
        else:
            joined.append(
                jnp.where(index == h, far, jnp.where(index > h, near[h], near[h - 1]))
            )
    return joined


def heads_of(ref):
    return [ref[:, h * HD : (h + 1) * HD].astype(jnp.float32) for h in range(NEAR + 1)]


def rounded(array):
    return array.astype(jnp.bfloat16).astype(jnp.float32)


def square_row(heads):
    total = heads[0] * heads[0]
    for part in heads[1:]:
        total = total + part * part
    column = jnp.sum(total, axis=1, keepdims=True)
    return jnp.broadcast_to(column, total.shape).T[0:1, :]


def store_near(ref, near, rows):
    for g in range(NEAR):
        ref[0:rows, g * HD : (g + 1) * HD] = near[g].astype(jnp.bfloat16)


def place(coordinate, ctx_count):
    return {"ctx": lax.rem(coordinate + ctx_count, ctx_count)}


def gather_kernel(
    ctx_count, head_total, kind_ref, q_ref, k_ref, v_ref, g_ref, qgain_ref, kgain_ref,
    qs_ref, ks_ref, vs_ref, gs_ref, far_ref,
    sums, far_out, ring_send, ring_recv, norm_send, norm_recv, far_send, far_recv,
):
    rows = q_ref.shape[0]
    reach = WINDOW // rows
    period = STRIDE // rows
    classes = ctx_count // period
    per_peer = rows // classes
    ctx = lax.axis_index("ctx")
    head = lax.axis_index("head")
    column = lax.rem(ctx, period)
    turn = lax.div(ctx, period)

    right = place(ctx + 1, ctx_count)
    left = place(ctx - 1, ctx_count)
    norm_peers = [lax.rem(head + t, head_total) for t in range(1, head_total)]
    far_peers = [lax.rem(turn + t, classes) * period + column for t in range(1, classes)]

    barrier = pltpu.get_barrier_semaphore()
    greeted = [right, left] + [{"head": p} for p in norm_peers] + [{"ctx": p} for p in far_peers]
    for peer in greeted:
        pl.semaphore_signal(barrier, inc=1, device_id=peer, device_id_type=MESH)

    index = strided_index(kind_ref)
    near_v, far_v = split_heads(heads_of(v_ref), index)
    near_g, far_g = split_heads(heads_of(g_ref), index)
    store_near(vs_ref, near_v, rows)
    store_near(gs_ref, near_g, rows)
    q_heads = heads_of(q_ref)
    k_heads = heads_of(k_ref)
    sums[head] = jnp.concatenate(
        [square_row(q_heads), square_row(k_heads), jnp.zeros((6, HD), jnp.float32)], axis=0
    )
    pl.semaphore_wait(barrier, len(greeted))

    def hop(which, ref, step, peer):
        return pltpu.make_async_remote_copy(
            src_ref=ref.at[pl.ds((step - 1) * rows, rows)],
            dst_ref=ref.at[pl.ds(step * rows, rows)],
            send_sem=ring_send.at[which, step - 1],
            recv_sem=ring_recv.at[which, step - 1],
            device_id=peer,
            device_id_type=MESH,
        )

    rings = [(0, vs_ref, right), (1, gs_ref, left), (2, ks_ref, right), (3, qs_ref, left)]
    hops = {
        (which, step): hop(which, ref, step, peer)
        for which, ref, peer in rings
        for step in range(1, reach + 1)
    }
    norm_copies = []
    for t in range(1, head_total):
        copy = pltpu.make_async_remote_copy(
            src_ref=sums.at[head],
            dst_ref=sums.at[head],
            send_sem=norm_send.at[t],
            recv_sem=norm_recv.at[t],
            device_id={"head": norm_peers[t - 1]},
            device_id_type=MESH,
        )
        copy.start()
        norm_copies.append(copy)
    hops[0, 1].start()
    hops[1, 1].start()

    for copy in norm_copies:
        copy.wait_recv()
    total = sums[0]
    for h in range(1, head_total):
        total = total + sums[h]
    inverse = lax.rsqrt(total / (head_total * (NEAR + 1) * HD) + EPSILON)
    q_scale = jnp.broadcast_to(inverse[0:1, :], (rows, rows)).T
    k_scale = jnp.broadcast_to(inverse[1:2, :], (rows, rows)).T
    q_normed = [
        rounded(part * q_scale * qgain_ref[:, h * HD : (h + 1) * HD])
        for h, part in enumerate(q_heads)
    ]
    k_normed = [
        rounded(part * k_scale * kgain_ref[:, h * HD : (h + 1) * HD])
        for h, part in enumerate(k_heads)
    ]
    near_q, far_q = split_heads(q_normed, index)
    near_k, far_k = split_heads(k_normed, index)
    store_near(ks_ref, near_k, rows)
    store_near(qs_ref, near_q, rows)
    packed = jnp.concatenate(
        [part.reshape(classes, per_peer, HD) for part in (far_q, far_k, far_v, far_g)], axis=1
    )
    far_out[...] = packed.astype(jnp.bfloat16)
    hops[2, 1].start()
    hops[3, 1].start()
    far_copies = []
    for t in range(1, classes):
        copy = pltpu.make_async_remote_copy(
            src_ref=far_out.at[lax.rem(turn + t, classes)],
            dst_ref=far_ref.at[turn],
            send_sem=far_send.at[t],
            recv_sem=far_recv.at[t],
            device_id={"ctx": far_peers[t - 1]},
            device_id_type=MESH,
        )
        copy.start()
        far_copies.append(copy)
    far_ref[turn] = far_out[turn]

    for step in range(1, reach + 1):
        for which, _, _ in rings:
            hops[which, step].wait_recv()
            if step < reach:
                hops[which, step + 1].start()
    for copy in far_copies:
        copy.wait_recv()
    for copy in far_copies + norm_copies + list(hops.values()):
        copy.wait_send()


def local_query_kernel(ctx_count, q_ref, k_ref, v_ref, g_ref, far_ref, dq_ref, stats_ref, far_out):
    span = k_ref.shape[0]
    rows = q_ref.shape[0]
    ctx = lax.axis_index("ctx")
    r = lax.broadcasted_iota(jnp.int32, (span, rows), 0)
    i = lax.broadcasted_iota(jnp.int32, (span, rows), 1)
    block = lax.shift_right_logical(r, int(math.log2(rows)))
    gap = i + block * (2 * rows) - r
    allowed = (gap >= 0) & (gap < WINDOW) & (block <= ctx)
    log_rows, delta_rows = [], []
    for h in range(NEAR):
        cut = slice(h * HD, (h + 1) * HD)
        dq, _, _, log_total, delta = attend(
            q_ref[:, cut], k_ref[:, cut], v_ref[:, cut], g_ref[:, cut], allowed, False
        )
        dq_ref[:, cut] = dq.astype(jnp.bfloat16)
        log_rows.append(log_total)
        delta_rows.append(delta)
    stats_ref[...] = jnp.concatenate(
        log_rows + delta_rows + [jnp.zeros((2, rows), jnp.float32)], axis=0
    )
    classes, quad, _ = far_ref.shape
    per_peer = quad // 4
    gathered = far_ref[...].astype(jnp.float32)
    far_q, far_k, far_v, far_g = [
        gathered[:, a * per_peer : (a + 1) * per_peer, :].reshape(rows, HD).astype(jnp.bfloat16)
        for a in range(4)
    ]
    j = lax.broadcasted_iota(jnp.int32, (rows, rows), 0)
    i = lax.broadcasted_iota(jnp.int32, (rows, rows), 1)
    far_allowed = (j <= i) & (((i - j) & (per_peer - 1)) == 0)
    dq, dk, dv, _, _ = attend(far_q, far_k, far_v, far_g, far_allowed, True)
    parts = [part.reshape(classes, per_peer, HD) for part in (dq, dk, dv, jnp.zeros_like(dq))]
    far_out[...] = jnp.concatenate(parts, axis=1).astype(jnp.bfloat16)


def attend(q, k, v, g, allowed, with_keys):
    scores = jnp.where(allowed, dot_nt(k, q) * SCORE_SCALE, -jnp.inf)
    top = jnp.max(scores, axis=0, keepdims=True)
    grown = jnp.exp(scores - top)
    total = jnp.sum(grown, axis=0, keepdims=True)
    weights = grown * (1.0 / total)
    weights_low = weights.astype(jnp.bfloat16)
    weight_grads = dot_nt(v, g)
    delta = jnp.sum(weights_low.astype(jnp.float32) * weight_grads, axis=0, keepdims=True)
    score_low = (weights * (weight_grads - delta)).astype(jnp.bfloat16)
    dq = dot_tn(score_low, k) * SCORE_SCALE
    log_total = top + jnp.log(total)
    if not with_keys:
        return dq, None, None, log_total, delta
    return dq, dot_nn(score_low, q) * SCORE_SCALE, dot_nn(weights_low, g), log_total, delta


def return_kernel(
    ctx_count, stats_ref, far_ref, all_stats, far_back, stat_send, stat_recv, far_send, far_recv
):
    classes = far_ref.shape[0]
    reach = all_stats.shape[0] - 1
    period = ctx_count // classes
    ctx = lax.axis_index("ctx")
    column = lax.rem(ctx, period)
    turn = lax.div(ctx, period)
    far_peers = [lax.rem(turn + t, classes) * period + column for t in range(1, classes)]
    barrier = pltpu.get_barrier_semaphore()
    greeted = [{"ctx": p} for p in far_peers]
    greeted += [place(ctx - o, ctx_count) for o in range(1, reach + 1)]
    greeted += [place(ctx + o, ctx_count) for o in range(1, reach + 1)]
    for peer in greeted:
        pl.semaphore_signal(barrier, inc=1, device_id=peer, device_id_type=MESH)
    all_stats[0] = stats_ref[...]
    far_back[turn] = far_ref[turn]
    pl.semaphore_wait(barrier, len(greeted))
    copies = []
    for t in range(1, classes):
        copies.append(
            pltpu.make_async_remote_copy(
                src_ref=far_ref.at[lax.rem(turn + t, classes)],
                dst_ref=far_back.at[turn],
                send_sem=far_send.at[t],
                recv_sem=far_recv.at[t],
                device_id={"ctx": far_peers[t - 1]},
                device_id_type=MESH,
            )
        )
    for o in range(1, reach + 1):
        copies.append(
            pltpu.make_async_remote_copy(
                src_ref=stats_ref,
                dst_ref=all_stats.at[o],
                send_sem=stat_send.at[o],
                recv_sem=stat_recv.at[o],
                device_id=place(ctx - o, ctx_count),
                device_id_type=MESH,
            )
        )
    for copy in copies:
        copy.start()
    for copy in copies:
        copy.wait_recv()
    for copy in copies:
        copy.wait_send()


def local_key_kernel(
    ctx_count, kind_ref, q_ref, k_ref, v_ref, g_ref, dq_ref, stats_ref, far_ref,
    q_out, k_out, v_out,
):
    rows = k_ref.shape[0]
    blocks = q_ref.shape[0] // rows
    ctx = lax.axis_index("ctx")
    index = strided_index(kind_ref)
    classes, quad, _ = far_ref.shape
    per_peer = quad // 4
    back = far_ref[...].astype(jnp.float32)
    far = [
        back[:, a * per_peer : (a + 1) * per_peer, :].reshape(rows, HD) for a in range(3)
    ]
    j = lax.broadcasted_iota(jnp.int32, (rows, rows), 0)
    i = lax.broadcasted_iota(jnp.int32, (rows, rows), 1)
    near_k, near_v = [], []
    for h in range(NEAR):
        cut = slice(h * HD, (h + 1) * HD)
        k = k_ref[:, cut]
        v = v_ref[:, cut]
        dk = jnp.zeros((rows, HD), jnp.float32)
        dv = jnp.zeros((rows, HD), jnp.float32)
        for o in range(blocks):
            q = q_ref[o * rows : (o + 1) * rows, cut]
            g = g_ref[o * rows : (o + 1) * rows, cut]
            gap = i - j + o * rows
            allowed = (gap >= 0) & (gap < WINDOW) & (i * 0 + (ctx + o) < ctx_count)
            log_row = stats_ref[o, h : h + 1, :]
            delta_row = stats_ref[o, NEAR + h : NEAR + h + 1, :]
            scores = dot_nt(k, q) * SCORE_SCALE
            weights = jnp.where(allowed, jnp.exp(scores - log_row), 0.0)
            score_grads = weights * (dot_nt(v, g) - delta_row)
            dv = dv + dot_nn(weights.astype(jnp.bfloat16), g)
            dk = dk + dot_nn(score_grads.astype(jnp.bfloat16), q)
        near_k.append(dk * SCORE_SCALE)
        near_v.append(dv)
    near_q = [dq_ref[:, h * HD : (h + 1) * HD].astype(jnp.float32) for h in range(NEAR)]
    for out, near, remote in ((q_out, near_q, far[0]), (k_out, near_k, far[1]), (v_out, near_v, far[2])):
        for h, part in enumerate(join_heads(near, remote, index)):
            out[:, h * HD : (h + 1) * HD] = part.astype(jnp.bfloat16)


def on_device(
    ctx_count, head_total, raw_queries, raw_keys, values, output_gradient, query_gain, key_gain, head_kind
):
    rows, width = raw_queries.shape
    reach = WINDOW // rows
    classes = ctx_count // (STRIDE // rows)
    quad = 4 * (rows // classes)
    near_width = NEAR * HD
    low, wide = jnp.bfloat16, jnp.float32
    vmem = pl.BlockSpec(memory_space=pltpu.VMEM)
    smem = pl.BlockSpec(memory_space=pltpu.SMEM)
    dma = pltpu.SemaphoreType.DMA
    span = jax.ShapeDtypeStruct(((reach + 1) * rows, near_width), low)
    far_shape = jax.ShapeDtypeStruct((classes, quad, HD), low)
    all_q, all_k, all_v, all_g, far_in = pl.pallas_call(
        functools.partial(gather_kernel, ctx_count, head_total),
        name="gather",
        out_shape=(span, span, span, span, far_shape),
        in_specs=[smem] + [vmem] * 6,
        out_specs=(vmem,) * 5,
        scratch_shapes=[
            pltpu.VMEM((head_total, 8, HD), wide),
            pltpu.VMEM((classes, quad, HD), low),
            dma((4, reach)),
            dma((4, reach)),
            dma((head_total,)),
            dma((head_total,)),
            dma((classes,)),
            dma((classes,)),
        ],
        compiler_params=pltpu.CompilerParams(collective_id=0, has_side_effects=True),
    )(
        head_kind, raw_queries, raw_keys, values, output_gradient,
        query_gain.reshape(1, width), key_gain.reshape(1, width),
    )
    first = pl.BlockSpec((rows, near_width), lambda s: (0, 0))
    full = pl.BlockSpec(span.shape, lambda s: (0, 0))
    cube = pl.BlockSpec(far_shape.shape, lambda s: (0, 0, 0))
    tile = pl.BlockSpec((8, HD), lambda s: (0, 0))
    near_dq, stats, far_result = pl.pallas_call(
        functools.partial(local_query_kernel, ctx_count),
        name="query_side",
        grid=(1,),
        out_shape=(
            jax.ShapeDtypeStruct((rows, near_width), low),
            jax.ShapeDtypeStruct((8, HD), wide),
            far_shape,
        ),
        in_specs=[first, full, full, first, cube],
        out_specs=(first, tile, cube),
    )(all_q, all_k, all_v, all_g, far_in)
    all_stats, far_back = pl.pallas_call(
        functools.partial(return_kernel, ctx_count),
        name="give_back",
        out_shape=(jax.ShapeDtypeStruct((reach + 1, 8, HD), wide), far_shape),
        in_specs=[vmem] * 2,
        out_specs=(vmem,) * 2,
        scratch_shapes=[dma((reach + 1,)), dma((reach + 1,)), dma((classes,)), dma((classes,))],
        compiler_params=pltpu.CompilerParams(collective_id=1, has_side_effects=True),
    )(stats, far_result)
    result = jax.ShapeDtypeStruct((rows, width), low)
    whole = pl.BlockSpec((rows, width), lambda s: (0, 0))
    return pl.pallas_call(
        functools.partial(local_key_kernel, ctx_count),
        name="key_side",
        grid=(1,),
        out_shape=(result,) * 3,
        in_specs=[
            smem, full, first, first, full, first,
            pl.BlockSpec((reach + 1, 8, HD), lambda s: (0, 0, 0)), cube,
        ],
        out_specs=(whole,) * 3,
    )(head_kind, all_q, all_k, all_v, all_g, near_dq, all_stats, far_back)


def solution(mesh):
    both = P("ctx", "head")
    placed = (both, both, both, both, P("head"), P("head"), P("head"))
    return jax.shard_map(
        functools.partial(on_device, mesh.shape["ctx"], mesh.shape["head"]),
        mesh=mesh,
        in_specs=placed,
        out_specs=(both, both, both),
        check_vma=False,
    )
```

time: 241 us -> 95.3 us (0.40)
  Pallas kernels: 0 us -> 93.8 us
  starting transfers between devices: 89.1 us -> 0 us
  waiting for transfers between devices: 72.8 us -> 0 us
  blocking collectives: 28.1 us -> 0 us
  local copies, waits for them, and re-layouts: 26.2 us -> 0 us
  matrix products: 11.1 us -> 0 us
  other arithmetic: 9.26 us -> 0 us
    pallas_call x0 -> x4, Pallas kernels: none -> 93.8 us  [the longest x1 66.9 us: on_device(): pl.pallas_call(functools.partial(gather_kernel, ctx_count, head_total), n...]
    ppermute x16 -> x0, waiting for transfers between devices: 62.2 us -> none  [from_behind(): return lax.ppermute(shard, axis, pairs)]
    ppermute x16 -> x0, starting transfers between devices: 49.7 us -> none  [from_behind(): return lax.ppermute(shard, axis, pairs)]
    all_to_all x2 -> x0, starting transfers between devices: 39.4 us -> none  [the longest x1 28.7 us: on_device(): lax.all_to_all(result, 'ctx', split_axis=1, concat_axis=1, tiled=True)]
    psum x1 -> x0, blocking collectives: 28.1 us -> none  [on_device(): lax.psum((jnp.sum(query_f * query_f, axis=1), jnp.sum(key_f * key_f, axis...]
    dot_general x14 -> x0, matrix products: 11.1 us -> none  [the longest x1 2.75 us: on_device(): jnp.einsum('hij,ihd->jhd', score_low, near_queries, preferred_element_typ...]
    all_to_all x2 -> x0, waiting for transfers between devices: 10.5 us -> none  [the longest x1 10.5 us: on_device(): lax.all_to_all(result, 'ctx', split_axis=1, concat_axis=1, tiled=True)]
    another operation x10 -> x0, local copies, waits for them, and re-layouts: 7.76 us -> none  [the longest x3 4.77 us: on_device(): jnp.stack([key_terms, value_terms])]
  transfers between devices with their start and end apart: 18 -> 0, of which waited for: 7 -> 0; matrix products, arithmetic and copies ran while one was open for 13% -> 0% of each run, Pallas kernels for 0% -> 0%
where the time goes in v1:
time: 95.3 us; the launch traced here: 94.5 us
  Pallas kernels  93.8 us (98%)
    pallas_call x1, Pallas kernels, on_device(): pl.pallas_call(functools.partial(gather_kernel, ctx_count, head_total), n...  66.9 us
    pallas_call x1, Pallas kernels, on_device(): pl.pallas_call(functools.partial(return_kernel, ctx_count), name='give_ba...  15.1 us
    pallas_call x1, Pallas kernels, on_device(): pl.pallas_call(functools.partial(local_key_kernel, ctx_count), name='key_...  6.76 us
    pallas_call x1, Pallas kernels, on_device(): pl.pallas_call(functools.partial(local_query_kernel, ctx_count), name='qu...  5.09 us

profile of v1, /device:TPU:14, one launch (start us, length us, event | category | flops | bytes accessed | tf_op | source)
XLA Modules:
  0.0 94.5 jit_solution(1675673574692832823)
XLA Ops:
  0.6 66.9 %gather.1 = (bf16[1152,384]{1,0:T(8,128)(2,1)}, bf16[1152,384]{1,0:T(8,128)(2,1)}, bf16[1152,384]{1,0:T(8,128)(2,1)}, bf16[1152,384]{1,0:T(8,128)(2,1)}, bf16[16,32,128]{2,1,0:T(8,128)(2,1)}) custom-call(s32[4]{0:T(128)} %kind_ref.3, bf16[128,512]{1,0:T(8,128)(2,1)} %q_ref.1, bf16[128,512]{1,0:T(8,128)(2,1)} %k_ref.1, bf16[128,512]{1,0:T(8,128)(2,1)} %v_ref.1, ...), custom_call_target="tpu_custom_call" | custom-call | tf_op jit(solution)/shard_map/gather/pallas_call | solution.py:364
  67.5 5.1 %query_side.1 = (bf16[128,384]{1,0:T(8,128)(2,1)}, f32[8,128]{1,0:T(8,128)}, bf16[16,32,128]{2,1,0:T(8,128)(2,1)}) custom-call(bf16[1152,384]{1,0:T(8,128)(2,1)} %get-tuple-element.13.q_ref, bf16[1152,384]{1,0:T(8,128)(2,1)} %get-tuple-element.14.k_ref, bf16[1152,384]{1,0:T(8,128)(2,1)} %get-tuple-element.15.v_ref, ...), custom_call_target="tpu_custom_call" | custom-call | tf_op jit(solution)/shard_map/query_side/pallas_call | solution.py:389
  72.6 15.1 %give_back.1 = (f32[9,8,128]{2,1,0:T(8,128)}, bf16[16,32,128]{2,1,0:T(8,128)(2,1)}) custom-call(f32[8,128]{1,0:T(8,128)} %get-tuple-element.19.stats_ref, bf16[16,32,128]{2,1,0:T(8,128)(2,1)} %get-tuple-element.20.far_ref), custom_call_target="tpu_custom_call" | custom-call | tf_op jit(solution)/shard_map/give_back/pallas_call | solution.py:401
  87.7 6.8 %key_side.1 = (bf16[128,512]{1,0:T(8,128)(2,1)}, bf16[128,512]{1,0:T(8,128)(2,1)}, bf16[128,512]{1,0:T(8,128)(2,1)}) custom-call(s32[4]{0:T(128)} %kind_ref.3, bf16[1152,384]{1,0:T(8,128)(2,1)} %get-tuple-element.13.q_ref, bf16[1152,384]{1,0:T(8,128)(2,1)} %get-tuple-element.14.k_ref, bf16[1152,384]{1,0:T(8,128)(2,1)} %get-tuple-element.15.v_ref, ...), custom_call_target="tpu_custom_call" | custom-call | tf_op jit(solution)/shard_map/key_side/pallas_call | solution.py:412

commit v2 on v0

v2 whole, which is shorter than its diff:
```python
import functools
import math

import jax
import jax.numpy as jnp
from jax import lax
from jax.experimental import pallas as pl
from jax.experimental.pallas import tpu as pltpu
from jax.sharding import PartitionSpec as P

HD = 128
WINDOW = 1024
STRIDE = 1024
EPSILON = 1e-06
NEAR = 3
MESH = pl.DeviceIdType.MESH
SCORE_SCALE = 1.0 / math.sqrt(HD)


def dot_nt(a, b):
    return lax.dot_general(a, b, (((1,), (1,)), ((), ())), preferred_element_type=jnp.float32)


def dot_tn(a, b):
    return lax.dot_general(a, b, (((0,), (0,)), ((), ())), preferred_element_type=jnp.float32)


def dot_nn(a, b):
    return lax.dot_general(a, b, (((1,), (0,)), ((), ())), preferred_element_type=jnp.float32)


def strided_index(kind_ref):
    index = kind_ref[1] + 2 * kind_ref[2] + 3 * kind_ref[3]
    return jnp.full((1, HD), index, jnp.int32)


def split_heads(heads, index):
    near = [jnp.where(index > g, heads[g], heads[g + 1]) for g in range(NEAR)]
    far = heads[NEAR]
    for g in range(NEAR):
        far = jnp.where(index == g, heads[g], far)
    return near, far


def join_heads(near, far, index):
    joined = []
    for h in range(NEAR + 1):
        if h == 0:
            kept = near[0]
            joined.append(jnp.where(index == 0, far, kept))
        elif h == NEAR:
            joined.append(jnp.where(index == h, far, near[h - 1]))
        else:
            joined.append(
                jnp.where(index == h, far, jnp.where(index > h, near[h], near[h - 1]))
            )
    return joined


def heads_of(ref):
    return [ref[:, h * HD : (h + 1) * HD].astype(jnp.float32) for h in range(NEAR + 1)]


def rounded(array):
    return array.astype(jnp.bfloat16).astype(jnp.float32)


def square_row(heads):
    total = heads[0] * heads[0]
    for part in heads[1:]:
        total = total + part * part
    column = jnp.sum(total, axis=1, keepdims=True)
    return jnp.broadcast_to(column, total.shape).T[0:1, :]


def store_near(ref, near, rows):
    for g in range(NEAR):
        ref[0:rows, g * HD : (g + 1) * HD] = near[g].astype(jnp.bfloat16)


def place(coordinate, ctx_count):
    return {"ctx": lax.rem(coordinate + ctx_count, ctx_count)}


def attend(q, k, v, g, allowed):
    scores = jnp.where(allowed, dot_nt(k, q) * SCORE_SCALE, -jnp.inf)
    top = jnp.max(scores, axis=0, keepdims=True)
    grown = jnp.exp(scores - top)
    total = jnp.sum(grown, axis=0, keepdims=True)
    weights = grown * (1.0 / total)
    weights_low = weights.astype(jnp.bfloat16)
    weight_grads = dot_nt(v, g)
    delta = jnp.sum(weights_low.astype(jnp.float32) * weight_grads, axis=0, keepdims=True)
    score_low = (weights * (weight_grads - delta)).astype(jnp.bfloat16)
    dq = dot_tn(score_low, k) * SCORE_SCALE
    return dq, score_low, weights_low, top + jnp.log(total), delta


def backward_kernel(
    ctx_count, head_total, kind_ref, q_ref, k_ref, v_ref, g_ref, qgain_ref, kgain_ref,
    q_out, k_out, v_out,
    qs, ks, vs, gs, sums, stats, far_out, far_in, far_res, far_back, dq_near, dk_near, dv_near,
    ring_send, ring_recv, norm_send, norm_recv, far_send, far_recv, back_send, back_recv,
    stat_send, stat_recv,
):
    rows = q_ref.shape[0]
    reach = WINDOW // rows
    half = reach // 2
    period = STRIDE // rows
    classes = ctx_count // period
    per_peer = rows // classes
    ctx = lax.axis_index("ctx")
    head = lax.axis_index("head")
    column = lax.rem(ctx, period)
    turn = lax.div(ctx, period)
    norm_peers = [{"head": lax.rem(head + t, head_total)} for t in range(1, head_total)]
    far_turns = [lax.rem(turn + t, classes) for t in range(1, classes)]
    far_peers = [{"ctx": t * period + column} for t in far_turns]
    ahead = [place(ctx + o, ctx_count) for o in range(1, reach + 1)]
    behind = [place(ctx - o, ctx_count) for o in range(1, reach + 1)]

    barrier = pltpu.get_barrier_semaphore()
    greeted = ahead + behind + norm_peers + far_peers
    for peer in greeted:
        pl.semaphore_signal(barrier, inc=1, device_id=peer, device_id_type=MESH)

    index = strided_index(kind_ref)
    near_v, far_v = split_heads(heads_of(v_ref), index)
    near_g, far_g = split_heads(heads_of(g_ref), index)
    store_near(vs, near_v, rows)
    store_near(gs, near_g, rows)
    q_heads = heads_of(q_ref)
    k_heads = heads_of(k_ref)
    sums[head] = jnp.concatenate(
        [square_row(q_heads), square_row(k_heads), jnp.zeros((6, HD), jnp.float32)], axis=0
    )
    stats[0] = jnp.zeros((8, HD), jnp.float32)
    pl.semaphore_wait(barrier, len(greeted))

    def remote(src, dst, send_sem, recv_sem, peer):
        return pltpu.make_async_remote_copy(
            src_ref=src, dst_ref=dst, send_sem=send_sem, recv_sem=recv_sem,
            device_id=peer, device_id_type=MESH,
        )

    values, grads, keys, queries = range(4)
    hops = {}
    for which, ref, forward in (
        (values, vs, True), (grads, gs, False), (keys, ks, True), (queries, qs, False)
    ):
        onward, backward = (ahead, behind) if forward else (behind, ahead)
        for slot in range(1, reach + 1):
            if slot <= half:
                source, peer = slot - 1, onward[0]
            elif slot == reach:
                source, peer = 0, onward[reach - 1]
            else:
                source, peer = slot + 1, backward[0]
            hops[which, slot] = remote(
                ref.at[pl.ds(source * rows, rows)],
                ref.at[pl.ds(slot * rows, rows)],
                ring_send.at[which, slot - 1],
                ring_recv.at[which, slot - 1],
                peer,
            )

    def launch(which):
        hops[which, reach].start()
        hops[which, 1].start()

    def advance(which, step):
        hops[which, step].wait_recv()
        if step < half:
            hops[which, step + 1].start()
        hops[which, reach + 1 - step].wait_recv()
        if reach + 1 - step > half + 1:
            hops[which, reach - step].start()

    norm_copies = [
        remote(sums.at[head], sums.at[head], norm_send.at[t + 1], norm_recv.at[t + 1], peer)
        for t, peer in enumerate(norm_peers)
    ]
    for copy in norm_copies:
        copy.start()
    launch(values)
    launch(grads)

    for copy in norm_copies:
        copy.wait_recv()
    total = sums[0]
    for h in range(1, head_total):
        total = total + sums[h]
    inverse = lax.rsqrt(total / (head_total * (NEAR + 1) * HD) + EPSILON)
    q_scale = jnp.broadcast_to(inverse[0:1, :], (rows, rows)).T
    k_scale = jnp.broadcast_to(inverse[1:2, :], (rows, rows)).T
    k_normed = [
        rounded(part * k_scale * kgain_ref[:, h * HD : (h + 1) * HD])
        for h, part in enumerate(k_heads)
    ]
    near_k, far_k = split_heads(k_normed, index)
    store_near(ks, near_k, rows)
    q_normed = [
        rounded(part * q_scale * qgain_ref[:, h * HD : (h + 1) * HD])
        for h, part in enumerate(q_heads)
    ]
    near_q, far_q = split_heads(q_normed, index)
    store_near(qs, near_q, rows)
    launch(keys)
    packed = jnp.concatenate(
        [part.reshape(classes, per_peer, HD) for part in (far_q, far_k, far_v, far_g)], axis=1
    )
    far_out[...] = packed.astype(jnp.bfloat16)
    advance(values, 1)
    advance(grads, 1)
    far_copies = [
        remote(far_out.at[far_turns[t]], far_in.at[turn], far_send.at[t + 1], far_recv.at[t + 1], peer)
        for t, peer in enumerate(far_peers)
    ]
    for copy in far_copies:
        copy.start()
    far_in[turn] = far_out[turn]
    advance(keys, 1)
    launch(queries)
    advance(values, 2)
    advance(grads, 2)
    advance(keys, 2)

    for copy in far_copies:
        copy.wait_recv()
    gathered = far_in[...].astype(jnp.float32)
    far_q, far_k, far_v, far_g = [
        gathered[:, a * per_peer : (a + 1) * per_peer, :].reshape(rows, HD).astype(jnp.bfloat16)
        for a in range(4)
    ]
    j = lax.broadcasted_iota(jnp.int32, (rows, rows), 0)
    i = lax.broadcasted_iota(jnp.int32, (rows, rows), 1)
    far_allowed = (j <= i) & (((i - j) & (per_peer - 1)) == 0)
    dq, score_low, weights_low, _, _ = attend(far_q, far_k, far_v, far_g, far_allowed)
    parts = [dq, dot_nn(score_low, far_q) * SCORE_SCALE, dot_nn(weights_low, far_g), jnp.zeros_like(dq)]
    far_res[...] = jnp.concatenate(
        [part.reshape(classes, per_peer, HD) for part in parts], axis=1
    ).astype(jnp.bfloat16)

    advance(values, 3)
    advance(grads, 3)
    advance(keys, 3)
    advance(queries, 1)
    back_copies = [
        remote(far_res.at[far_turns[t]], far_back.at[turn], back_send.at[t + 1], back_recv.at[t + 1], peer)
        for t, peer in enumerate(far_peers)
    ]
    for copy in back_copies:
        copy.start()
    far_back[turn] = far_res[turn]
    advance(values, 4)
    advance(keys, 4)

    span = (reach + 1) * rows

    def query_side(h):
        r = lax.broadcasted_iota(jnp.int32, (span, rows), 0)
        c = lax.broadcasted_iota(jnp.int32, (span, rows), 1)
        block = lax.shift_right_logical(r, int(math.log2(rows)))
        gap = c + block * (2 * rows) - r
        allowed = (gap >= 0) & (gap < WINDOW) & (block <= ctx)
        cut = slice(h * HD, (h + 1) * HD)
        dq, _, _, log_total, delta = attend(
            qs[0:rows, cut], ks[:, cut], vs[:, cut], gs[0:rows, cut], allowed
        )
        dq_near[:, cut] = dq
        stats[0, h : h + 1, :] = log_total
        stats[0, NEAR + h : NEAR + h + 1, :] = delta

    def key_side(o):
        gap = i - j + o * rows
        allowed = (gap >= 0) & (gap < WINDOW) & (i * 0 + (ctx + o) < ctx_count)
        for h in range(NEAR):
            cut = slice(h * HD, (h + 1) * HD)
            q = qs[o * rows : (o + 1) * rows, cut]
            g = gs[o * rows : (o + 1) * rows, cut]
            scores = dot_nt(ks[0:rows, cut], q) * SCORE_SCALE
            weights = jnp.where(allowed, jnp.exp(scores - stats[o, h : h + 1, :]), 0.0)
            score_grads = weights * (
                dot_nt(vs[0:rows, cut], g) - stats[o, NEAR + h : NEAR + h + 1, :]
            )
            dv = dot_nn(weights.astype(jnp.bfloat16), g)
            dk = dot_nn(score_grads.astype(jnp.bfloat16), q)
            if o == 0:
                dv_near[:, cut] = dv
                dk_near[:, cut] = dk
            else:
                dv_near[:, cut] += dv
                dk_near[:, cut] += dk

    query_side(0)
    advance(queries, 2)
    query_side(1)
    advance(queries, 3)
    query_side(2)
    advance(grads, 4)
    stat_copies = {
        o: remote(stats.at[0], stats.at[o], stat_send.at[o], stat_recv.at[o], behind[o - 1])
        for o in range(1, reach + 1)
    }
    for copy in stat_copies.values():
        copy.start()
    key_side(0)

    for copy in back_copies:
        copy.wait_recv()
    back = far_back[...].astype(jnp.float32)
    far = [back[:, a * per_peer : (a + 1) * per_peer, :].reshape(rows, HD) for a in range(3)]

    def put(out, near_ref, remote_part, scale):
        near = [near_ref[:, h * HD : (h + 1) * HD] * scale for h in range(NEAR)]
        for h, part in enumerate(join_heads(near, remote_part, index)):
            out[:, h * HD : (h + 1) * HD] = part.astype(jnp.bfloat16)

    put(q_out, dq_near, far[0], 1.0)
    order = []
    for step in range(1, half):
        order += [step, reach + 1 - step]
    for o in order:
        stat_copies[o].wait_recv()
        key_side(o)
    advance(queries, 4)
    for o in (half, half + 1):
        stat_copies[o].wait_recv()
        key_side(o)
    put(k_out, dk_near, far[1], SCORE_SCALE)
    put(v_out, dv_near, far[2], 1.0)
    sent = norm_copies + far_copies + back_copies + list(stat_copies.values()) + list(hops.values())
    for copy in sent:
        copy.wait_send()


def on_device(
    ctx_count, head_total, raw_queries, raw_keys, values, output_gradient, query_gain, key_gain, head_kind
):
    rows, width = raw_queries.shape
    reach = WINDOW // rows
    classes = ctx_count // (STRIDE // rows)
    quad = 4 * (rows // classes)
    near_width = NEAR * HD
    low, wide = jnp.bfloat16, jnp.float32
    vmem = pl.BlockSpec(memory_space=pltpu.VMEM)
    smem = pl.BlockSpec(memory_space=pltpu.SMEM)
    dma = pltpu.SemaphoreType.DMA
    result = jax.ShapeDtypeStruct((rows, width), low)
    return pl.pallas_call(
        functools.partial(backward_kernel, ctx_count, head_total),
        name="backward",
        out_shape=(result,) * 3,
        in_specs=[smem] + [vmem] * 6,
        out_specs=(vmem,) * 3,
        scratch_shapes=[pltpu.VMEM(((reach + 1) * rows, near_width), low)] * 4
        + [
            pltpu.VMEM((head_total, 8, HD), wide),
            pltpu.VMEM((reach + 1, 8, HD), wide),
        ]
        + [pltpu.VMEM((classes, quad, HD), low)] * 4
        + [pltpu.VMEM((rows, near_width), wide)] * 3
        + [dma((4, reach))] * 2
        + [dma((head_total,))] * 2
        + [dma((classes,))] * 4
        + [dma((reach + 1,))] * 2,
        compiler_params=pltpu.CompilerParams(collective_id=0, has_side_effects=True),
    )(
        head_kind, raw_queries, raw_keys, values, output_gradient,
        query_gain.reshape(1, width), key_gain.reshape(1, width),
    )


def solution(mesh):
    both = P("ctx", "head")
    placed = (both, both, both, both, P("head"), P("head"), P("head"))
    return jax.shard_map(
        functools.partial(on_device, mesh.shape["ctx"], mesh.shape["head"]),
        mesh=mesh,
        in_specs=placed,
        out_specs=(both, both, both),
        check_vma=False,
    )
```

time: 241 us -> 93 us (0.39); the launches traced: 238 us -> 92.8 us
  starting transfers between devices: 89.1 us -> 0 us
  Pallas kernels: 0 us -> 88.9 us
  waiting for transfers between devices: 72.8 us -> 0 us
  blocking collectives: 28.1 us -> 0 us
  local copies, waits for them, and re-layouts: 26.2 us -> 3.21 us
  matrix products: 11.1 us -> 0 us
  other arithmetic: 9.26 us -> 0 us
    pallas_call x0 -> x1, Pallas kernels: none -> 88.9 us  [on_device(): pl.pallas_call(functools.partial(backward_kernel, ctx_count, head_total),...]
    ppermute x16 -> x0, waiting for transfers between devices: 62.2 us -> none  [from_behind(): return lax.ppermute(shard, axis, pairs)]
    ppermute x16 -> x0, starting transfers between devices: 49.7 us -> none  [from_behind(): return lax.ppermute(shard, axis, pairs)]
    all_to_all x2 -> x0, starting transfers between devices: 39.4 us -> none  [the longest x1 28.7 us: on_device(): lax.all_to_all(result, 'ctx', split_axis=1, concat_axis=1, tiled=True)]
    psum x1 -> x0, blocking collectives: 28.1 us -> none  [on_device(): lax.psum((jnp.sum(query_f * query_f, axis=1), jnp.sum(key_f * key_f, axis...]
    dot_general x14 -> x0, matrix products: 11.1 us -> none  [the longest x1 2.75 us: on_device(): jnp.einsum('hij,ihd->jhd', score_low, near_queries, preferred_element_typ...]
    all_to_all x2 -> x0, waiting for transfers between devices: 10.5 us -> none  [the longest x1 10.5 us: on_device(): lax.all_to_all(result, 'ctx', split_axis=1, concat_axis=1, tiled=True)]
    another operation x10 -> x0, local copies, waits for them, and re-layouts: 7.76 us -> none  [the longest x3 4.77 us: on_device(): jnp.stack([key_terms, value_terms])]
  transfers between devices with their start and end apart: 18 -> 0, of which waited for: 7 -> 0; matrix products, arithmetic and copies ran while one was open for 13% -> 0% of each run, Pallas kernels for 0% -> 0%
where the time goes in v2:
time: 93 us; the launch traced here: 92.8 us
  Pallas kernels  88.9 us (96%)
  local copies, waits for them, and re-layouts  3.21 us (3%)
    pallas_call x1, Pallas kernels, on_device(): pl.pallas_call(functools.partial(backward_kernel, ctx_count, head_total),...  88.9 us
    unnamed x7, local copies, waits for them, and re-layouts  3.21 us

profile of v2, /device:TPU:14, one launch (start us, length us, event | category | flops | bytes accessed | tf_op | source)
XLA Modules:
  0.0 92.8 jit_solution(11044516109541729981)
XLA Ops:
  0.6 88.9 %backward.1 = (bf16[128,512]{1,0:T(8,128)(2,1)}, bf16[128,512]{1,0:T(8,128)(2,1)}, bf16[128,512]{1,0:T(8,128)(2,1)}) custom-call(s32[4]{0:T(128)} %kind_ref.1, bf16[128,512]{1,0:T(8,128)(2,1)} %q_ref.1, bf16[128,512]{1,0:T(8,128)(2,1)} %k_ref.1, bf16[128,512]{1,0:T(8,128)(2,1)} %v_ref.1, bf16[128,512]{1,0:T(8,128)(2,1)} %g_ref.1, f32[1,512]{1,0:T(1,128)} %bitcast.2, ...), custom_call_target="tpu_custom_call" | custom-call | tf_op jit(solution)/shard_map/backward/pallas_call | solution.py:350
  89.5 0.0 copy-start.1
  89.5 1.6 %copy.13 = bf16[128,512]{1,0:T(8,128)(2,1)} copy(bf16[128,512]{1,0:T(8,128)(2,1)} %get-tuple-element.6) | data formatting | bytes 262144
  91.2 0.0 copy-done.1
  91.2 0.0 copy-start
  91.2 0.7 copy.14
  91.8 0.3 copy-done
  92.1 0.7 copy.15
Async XLA Ops:
  89.5 1.6 %copy-start.1 = (bf16[128,512]{1,0:T(8,128)(2,1)S(1)}, bf16[128,512]{1,0:T(8,128)(2,1)}, u32[]{:S(2)}) copy-start(bf16[128,512]{1,0:T(8,128)(2,1)} %get-tuple-element.7) | copy-start | bytes 393220
  91.2 1.0 %copy-start = (bf16[128,512]{1,0:T(8,128)(2,1)S(1)}, bf16[128,512]{1,0:T(8,128)(2,1)}, u32[]{:S(2)}) copy-start(bf16[128,512]{1,0:T(8,128)(2,1)} %get-tuple-element.8) | copy-start | bytes 393220

commit v3 on v2

--- a/solution.py
+++ b/solution.py
@@ -101,7 +101,7 @@
     q_out, k_out, v_out,
     qs, ks, vs, gs, sums, stats, far_out, far_in, far_res, far_back, dq_near, dk_near, dv_near,
     ring_send, ring_recv, norm_send, norm_recv, far_send, far_recv, back_send, back_recv,
-    stat_send, stat_recv,
+    stat_send, stat_recv, bounce, bounce_send, bounce_recv,
 ):
     rows = q_ref.shape[0]
     reach = WINDOW // rows
@@ -144,37 +144,80 @@
         )
 
     values, grads, keys, queries = range(4)
-    hops = {}
-    for which, ref, forward in (
-        (values, vs, True), (grads, gs, False), (keys, ks, True), (queries, qs, False)
+    first_column = column == 0
+    last_column = column == period - 1
+    hops, edges, passes = {}, {}, {}
+    for which, ref, forward, y_first in (
+        (values, vs, True, True),
+        (grads, gs, False, False),
+        (keys, ks, True, False),
+        (queries, qs, False, True),
     ):
         onward, backward = (ahead, behind) if forward else (behind, ahead)
         for slot in range(1, reach + 1):
-            if slot <= half:
-                source, peer = slot - 1, onward[0]
-            elif slot == reach:
-                source, peer = 0, onward[reach - 1]
-            else:
-                source, peer = slot + 1, backward[0]
-            hops[which, slot] = remote(
-                ref.at[pl.ds(source * rows, rows)],
-                ref.at[pl.ds(slot * rows, rows)],
-                ring_send.at[which, slot - 1],
-                ring_recv.at[which, slot - 1],
-                peer,
+            source = slot - 1 if slot <= half else (0 if slot == reach else slot + 1)
+            piece = ref.at[pl.ds(source * rows, rows)]
+            landing = ref.at[pl.ds(slot * rows, rows)]
+            send, recv = ring_send.at[which, slot - 1], ring_recv.at[which, slot - 1]
+            if slot == reach:
+                hops[which, slot] = remote(piece, landing, send, recv, onward[reach - 1])
+                continue
+            here, there = (onward, backward) if slot <= half else (backward, onward)
+            hops[which, slot] = remote(piece, landing, send, recv, here[0])
+            upward = here is ahead
+            near_edge, far_edge = (
+                (last_column, first_column) if upward else (first_column, last_column)
             )
+            by_row, by_column = here[period - 1], there[period - 2]
+            stop = bounce.at[which, slot - 1]
+            edges[which, slot] = (
+                near_edge,
+                remote(
+                    piece, stop, send, bounce_recv.at[which, slot - 1],
+                    by_row if y_first else by_column,
+                ),
+            )
+            passes[which, slot] = (
+                near_edge if y_first else far_edge,
+                remote(
+                    stop, landing, bounce_send.at[which, slot - 1], recv,
+                    by_column if y_first else by_row,
+                ),
+            )
+
+    def send_on(which, slot):
+        at_edge, copy = edges[which, slot]
+
+        @pl.when(at_edge)
+        def _():
+            copy.start()
+
+        @pl.when(jnp.logical_not(at_edge))
+        def _():
+            hops[which, slot].start()
+
+    def arrive(which, slot):
+        if slot < reach:
+            relays, copy = passes[which, slot]
+
+            @pl.when(relays)
+            def _():
+                edges[which, slot][1].wait_recv()
+                copy.start()
+
+        hops[which, slot].wait_recv()
 
     def launch(which):
         hops[which, reach].start()
-        hops[which, 1].start()
+        send_on(which, 1)
 
     def advance(which, step):
-        hops[which, step].wait_recv()
+        arrive(which, step)
         if step < half:
-            hops[which, step + 1].start()
-        hops[which, reach + 1 - step].wait_recv()
+            send_on(which, step + 1)
+        arrive(which, reach + 1 - step)
         if reach + 1 - step > half + 1:
-            hops[which, reach - step].start()
+            send_on(which, reach - step)
 
     norm_copies = [
         remote(sums.at[head], sums.at[head], norm_send.at[t + 1], norm_recv.at[t + 1], peer)
@@ -332,6 +375,8 @@
     sent = norm_copies + far_copies + back_copies + list(stat_copies.values()) + list(hops.values())
     for copy in sent:
         copy.wait_send()
+    for relays, copy in passes.values():
+        pl.when(relays)(copy.wait_send)
 
 
 def on_device(
@@ -363,7 +408,9 @@
         + [dma((4, reach))] * 2
         + [dma((head_total,))] * 2
         + [dma((classes,))] * 4
-        + [dma((reach + 1,))] * 2,
+        + [dma((reach + 1,))] * 2
+        + [pltpu.VMEM((4, reach - 1, rows, near_width), low)]
+        + [dma((4, reach - 1))] * 2,
         compiler_params=pltpu.CompilerParams(collective_id=0, has_side_effects=True),
     )(
         head_kind, raw_queries, raw_keys, values, output_gradient,

time: 93 us -> 134 us (1.44)
  the two profiles are of different devices: /device:TPU:14 before, /device:TPU:32 now
where the time goes in v3:
time: 134 us
  Pallas kernels  130 us (97%)
  local copies, waits for them, and re-layouts  3.21 us (2%)
    pallas_call x1, Pallas kernels, on_device(): pl.pallas_call(functools.partial(backward_kernel, ctx_count, head_total),...  130 us
    unnamed x7, local copies, waits for them, and re-layouts  3.21 us

profile of v3, /device:TPU:32, one launch (start us, length us, event | category | flops | bytes accessed | tf_op | source)
XLA Modules:
  0.0 134.0 jit_solution(316551764631167697)
XLA Ops:
  0.6 130.1 %backward.1 = (bf16[128,512]{1,0:T(8,128)(2,1)}, bf16[128,512]{1,0:T(8,128)(2,1)}, bf16[128,512]{1,0:T(8,128)(2,1)}) custom-call(s32[4]{0:T(128)} %kind_ref.1, bf16[128,512]{1,0:T(8,128)(2,1)} %q_ref.1, bf16[128,512]{1,0:T(8,128)(2,1)} %k_ref.1, bf16[128,512]{1,0:T(8,128)(2,1)} %v_ref.1, bf16[128,512]{1,0:T(8,128)(2,1)} %g_ref.1, f32[1,512]{1,0:T(1,128)} %bitcast.2, ...), custom_call_target="tpu_custom_call" | custom-call | tf_op jit(solution)/shard_map/backward/pallas_call | solution.py:395
  130.7 0.0 copy-start.1
  130.7 1.6 %copy.13 = bf16[128,512]{1,0:T(8,128)(2,1)} copy(bf16[128,512]{1,0:T(8,128)(2,1)} %get-tuple-element.6) | data formatting | bytes 262144
  132.3 0.0 copy-done.1
  132.3 0.0 copy-start
  132.4 0.7 copy.14
  133.0 0.3 copy-done
  133.3 0.7 copy.15
Async XLA Ops:
  130.7 1.6 %copy-start.1 = (bf16[128,512]{1,0:T(8,128)(2,1)S(1)}, bf16[128,512]{1,0:T(8,128)(2,1)}, u32[]{:S(2)}) copy-start(bf16[128,512]{1,0:T(8,128)(2,1)} %get-tuple-element.7) | copy-start | bytes 393220
  132.3 1.0 copy-start

commit v4 on v2

--- a/solution.py
+++ b/solution.py
@@ -83,13 +83,16 @@
 
 
 def attend(q, k, v, g, allowed):
-    scores = jnp.where(allowed, dot_nt(k, q) * SCORE_SCALE, -jnp.inf)
+    return weigh(dot_nt(k, q) * SCORE_SCALE, dot_nt(v, g), k, allowed)
+
+
+def weigh(scores, weight_grads, k, allowed):
+    scores = jnp.where(allowed, scores, -jnp.inf)
     top = jnp.max(scores, axis=0, keepdims=True)
     grown = jnp.exp(scores - top)
     total = jnp.sum(grown, axis=0, keepdims=True)
     weights = grown * (1.0 / total)
     weights_low = weights.astype(jnp.bfloat16)
-    weight_grads = dot_nt(v, g)
     delta = jnp.sum(weights_low.astype(jnp.float32) * weight_grads, axis=0, keepdims=True)
     score_low = (weights * (weight_grads - delta)).astype(jnp.bfloat16)
     dq = dot_tn(score_low, k) * SCORE_SCALE
@@ -101,11 +104,10 @@
     q_out, k_out, v_out,
     qs, ks, vs, gs, sums, stats, far_out, far_in, far_res, far_back, dq_near, dk_near, dv_near,
     ring_send, ring_recv, norm_send, norm_recv, far_send, far_recv, back_send, back_recv,
-    stat_send, stat_recv,
+    stat_send, stat_recv, query_scores, query_grads, key_scores, key_grads,
 ):
     rows = q_ref.shape[0]
     reach = WINDOW // rows
-    half = reach // 2
     period = STRIDE // rows
     classes = ctx_count // period
     per_peer = rows // classes
@@ -148,14 +150,9 @@
     for which, ref, forward in (
         (values, vs, True), (grads, gs, False), (keys, ks, True), (queries, qs, False)
     ):
-        onward, backward = (ahead, behind) if forward else (behind, ahead)
+        peer = ahead[0] if forward else behind[0]
         for slot in range(1, reach + 1):
-            if slot <= half:
-                source, peer = slot - 1, onward[0]
-            elif slot == reach:
-                source, peer = 0, onward[reach - 1]
-            else:
-                source, peer = slot + 1, backward[0]
+            source = slot - 1
             hops[which, slot] = remote(
                 ref.at[pl.ds(source * rows, rows)],
                 ref.at[pl.ds(slot * rows, rows)],
@@ -164,17 +161,10 @@
                 peer,
             )
 
-    def launch(which):
-        hops[which, reach].start()
-        hops[which, 1].start()
-
     def advance(which, step):
         hops[which, step].wait_recv()
-        if step < half:
+        if step < reach:
             hops[which, step + 1].start()
-        hops[which, reach + 1 - step].wait_recv()
-        if reach + 1 - step > half + 1:
-            hops[which, reach - step].start()
 
     norm_copies = [
         remote(sums.at[head], sums.at[head], norm_send.at[t + 1], norm_recv.at[t + 1], peer)
@@ -182,8 +172,8 @@
     ]
     for copy in norm_copies:
         copy.start()
-    launch(values)
-    launch(grads)
+    hops[values, 1].start()
+    hops[grads, 1].start()
 
     for copy in norm_copies:
         copy.wait_recv()
@@ -205,13 +195,12 @@
     ]
     near_q, far_q = split_heads(q_normed, index)
     store_near(qs, near_q, rows)
-    launch(keys)
+    hops[keys, 1].start()
+    hops[queries, 1].start()
     packed = jnp.concatenate(
         [part.reshape(classes, per_peer, HD) for part in (far_q, far_k, far_v, far_g)], axis=1
     )
     far_out[...] = packed.astype(jnp.bfloat16)
-    advance(values, 1)
-    advance(grads, 1)
     far_copies = [
         remote(far_out.at[far_turns[t]], far_in.at[turn], far_send.at[t + 1], far_recv.at[t + 1], peer)
         for t, peer in enumerate(far_peers)
@@ -219,11 +208,28 @@
     for copy in far_copies:
         copy.start()
     far_in[turn] = far_out[turn]
-    advance(keys, 1)
-    launch(queries)
-    advance(values, 2)
-    advance(grads, 2)
-    advance(keys, 2)
+    j = lax.broadcasted_iota(jnp.int32, (rows, rows), 0)
+    i = lax.broadcasted_iota(jnp.int32, (rows, rows), 1)
+    span = (reach + 1) * rows
+
+    def products(o):
+        block = slice(o * rows, (o + 1) * rows)
+        for h in range(NEAR):
+            cut = slice(h * HD, (h + 1) * HD)
+            own_q, own_k, own_v, own_g = qs[0:rows, cut], ks[0:rows, cut], vs[0:rows, cut], gs[0:rows, cut]
+            query_scores[h, block, :] = dot_nt(ks[block, cut], own_q) * SCORE_SCALE
+            query_grads[h, block, :] = dot_nt(vs[block, cut], own_g)
+            key_scores[h, block, :] = dot_nt(own_k, qs[block, cut]) * SCORE_SCALE
+            key_grads[h, block, :] = dot_nt(own_v, gs[block, cut])
+
+    def ring_step(step):
+        for which in (values, grads, keys, queries):
+            advance(which, step)
+        products(step)
+
+    products(0)
+    ring_step(1)
+    ring_step(2)
 
     for copy in far_copies:
         copy.wait_recv()
@@ -232,8 +238,6 @@
         gathered[:, a * per_peer : (a + 1) * per_peer, :].reshape(rows, HD).astype(jnp.bfloat16)
         for a in range(4)
     ]
-    j = lax.broadcasted_iota(jnp.int32, (rows, rows), 0)
-    i = lax.broadcasted_iota(jnp.int32, (rows, rows), 1)
     far_allowed = (j <= i) & (((i - j) & (per_peer - 1)) == 0)
     dq, score_low, weights_low, _, _ = attend(far_q, far_k, far_v, far_g, far_allowed)
     parts = [dq, dot_nn(score_low, far_q) * SCORE_SCALE, dot_nn(weights_low, far_g), jnp.zeros_like(dq)]
@@ -241,10 +245,7 @@
         [part.reshape(classes, per_peer, HD) for part in parts], axis=1
     ).astype(jnp.bfloat16)
 
-    advance(values, 3)
-    advance(grads, 3)
-    advance(keys, 3)
-    advance(queries, 1)
+    ring_step(3)
     back_copies = [
         remote(far_res.at[far_turns[t]], far_back.at[turn], back_send.at[t + 1], back_recv.at[t + 1], peer)
         for t, peer in enumerate(far_peers)
@@ -252,10 +253,8 @@
     for copy in back_copies:
         copy.start()
     far_back[turn] = far_res[turn]
-    advance(values, 4)
-    advance(keys, 4)
-
-    span = (reach + 1) * rows
+    for step in range(4, reach + 1):
+        ring_step(step)
 
     def query_side(h):
         r = lax.broadcasted_iota(jnp.int32, (span, rows), 0)
@@ -264,9 +263,7 @@
         gap = c + block * (2 * rows) - r
         allowed = (gap >= 0) & (gap < WINDOW) & (block <= ctx)
         cut = slice(h * HD, (h + 1) * HD)
-        dq, _, _, log_total, delta = attend(
-            qs[0:rows, cut], ks[:, cut], vs[:, cut], gs[0:rows, cut], allowed
-        )
+        dq, _, _, log_total, delta = weigh(query_scores[h], query_grads[h], ks[:, cut], allowed)
         dq_near[:, cut] = dq
         stats[0, h : h + 1, :] = log_total
         stats[0, NEAR + h : NEAR + h + 1, :] = delta
@@ -278,10 +275,10 @@
             cut = slice(h * HD, (h + 1) * HD)
             q = qs[o * rows : (o + 1) * rows, cut]
             g = gs[o * rows : (o + 1) * rows, cut]
-            scores = dot_nt(ks[0:rows, cut], q) * SCORE_SCALE
-            weights = jnp.where(allowed, jnp.exp(scores - stats[o, h : h + 1, :]), 0.0)
+            block = slice(o * rows, (o + 1) * rows)
+            weights = jnp.where(allowed, jnp.exp(key_scores[h, block, :] - stats[o, h : h + 1, :]), 0.0)
             score_grads = weights * (
-                dot_nt(vs[0:rows, cut], g) - stats[o, NEAR + h : NEAR + h + 1, :]
+                key_grads[h, block, :] - stats[o, NEAR + h : NEAR + h + 1, :]
             )
             dv = dot_nn(weights.astype(jnp.bfloat16), g)
             dk = dot_nn(score_grads.astype(jnp.bfloat16), q)
@@ -292,12 +289,19 @@
                 dv_near[:, cut] += dv
                 dk_near[:, cut] += dk
 
-    query_side(0)
-    advance(queries, 2)
-    query_side(1)
-    advance(queries, 3)
-    query_side(2)
-    advance(grads, 4)
+    for h in range(NEAR):
+        query_side(h)
+    for copy in back_copies:
+        copy.wait_recv()
+    back = far_back[...].astype(jnp.float32)
+    far = [back[:, a * per_peer : (a + 1) * per_peer, :].reshape(rows, HD) for a in range(3)]
+
+    def put(out, near_ref, remote_part, scale):
+        near = [near_ref[:, h * HD : (h + 1) * HD] * scale for h in range(NEAR)]
+        for h, part in enumerate(join_heads(near, remote_part, index)):
+            out[:, h * HD : (h + 1) * HD] = part.astype(jnp.bfloat16)
+
+    put(q_out, dq_near, far[0], 1.0)
     stat_copies = {
         o: remote(stats.at[0], stats.at[o], stat_send.at[o], stat_recv.at[o], behind[o - 1])
         for o in range(1, reach + 1)
@@ -306,25 +310,7 @@
         copy.start()
     key_side(0)
 
-    for copy in back_copies:
-        copy.wait_recv()
-    back = far_back[...].astype(jnp.float32)
-    far = [back[:, a * per_peer : (a + 1) * per_peer, :].reshape(rows, HD) for a in range(3)]
-
-    def put(out, near_ref, remote_part, scale):
-        near = [near_ref[:, h * HD : (h + 1) * HD] * scale for h in range(NEAR)]
-        for h, part in enumerate(join_heads(near, remote_part, index)):
-            out[:, h * HD : (h + 1) * HD] = part.astype(jnp.bfloat16)
-
-    put(q_out, dq_near, far[0], 1.0)
-    order = []
-    for step in range(1, half):
-        order += [step, reach + 1 - step]
-    for o in order:
-        stat_copies[o].wait_recv()
-        key_side(o)
-    advance(queries, 4)
-    for o in (half, half + 1):
+    for o in range(1, reach + 1):
         stat_copies[o].wait_recv()
         key_side(o)
     put(k_out, dk_near, far[1], SCORE_SCALE)
@@ -363,7 +349,8 @@
         + [dma((4, reach))] * 2
         + [dma((head_total,))] * 2
         + [dma((classes,))] * 4
-        + [dma((reach + 1,))] * 2,
+        + [dma((reach + 1,))] * 2
+        + [pltpu.VMEM((NEAR, (reach + 1) * rows, rows), wide)] * 4,
         compiler_params=pltpu.CompilerParams(collective_id=0, has_side_effects=True),
     )(
         head_kind, raw_queries, raw_keys, values, output_gradient,

time: 93 us -> 91 us (0.978)
  the two profiles are of different devices: /device:TPU:14 before, /device:TPU:114 now
where the time goes in v4:
time: 91 us; the launch traced here: 90.8 us
  Pallas kernels  87 us (96%)
  local copies, waits for them, and re-layouts  3.21 us (4%)
    pallas_call x1, Pallas kernels, on_device(): pl.pallas_call(functools.partial(backward_kernel, ctx_count, head_total),...  87 us
    unnamed x7, local copies, waits for them, and re-layouts  3.21 us

profile of v4, /device:TPU:114, one launch (start us, length us, event | category | flops | bytes accessed | tf_op | source)
XLA Modules:
  0.0 90.8 jit_solution(11923711698761302602)
XLA Ops:
  0.6 87.0 %backward.1 = (bf16[128,512]{1,0:T(8,128)(2,1)}, bf16[128,512]{1,0:T(8,128)(2,1)}, bf16[128,512]{1,0:T(8,128)(2,1)}) custom-call(s32[4]{0:T(128)} %kind_ref.1, bf16[128,512]{1,0:T(8,128)(2,1)} %q_ref.1, bf16[128,512]{1,0:T(8,128)(2,1)} %k_ref.1, bf16[128,512]{1,0:T(8,128)(2,1)} %v_ref.1, bf16[128,512]{1,0:T(8,128)(2,1)} %g_ref.1, f32[1,512]{1,0:T(1,128)} %bitcast.2, ...), custom_call_target="tpu_custom_call" | custom-call | tf_op jit(solution)/shard_map/backward/pallas_call | solution.py:336
  87.6 0.0 copy-start.1
  87.6 1.6 %copy.13 = bf16[128,512]{1,0:T(8,128)(2,1)} copy(bf16[128,512]{1,0:T(8,128)(2,1)} %get-tuple-element.6) | data formatting | bytes 262144
  89.2 0.0 copy-done.1
  89.2 0.0 copy-start
  89.2 0.7 copy.14
  89.9 0.3 copy-done
  90.2 0.7 copy.15
Async XLA Ops:
  87.6 1.6 %copy-start.1 = (bf16[128,512]{1,0:T(8,128)(2,1)S(1)}, bf16[128,512]{1,0:T(8,128)(2,1)}, u32[]{:S(2)}) copy-start(bf16[128,512]{1,0:T(8,128)(2,1)} %get-tuple-element.7) | copy-start | bytes 393220
  89.2 1.0 %copy-start = (bf16[128,512]{1,0:T(8,128)(2,1)S(1)}, bf16[128,512]{1,0:T(8,128)(2,1)}, u32[]{:S(2)}) copy-start(bf16[128,512]{1,0:T(8,128)(2,1)} %get-tuple-element.8) | copy-start | bytes 393220

commit v5 on v4

--- a/solution.py
+++ b/solution.py
@@ -13,6 +13,7 @@
 STRIDE = 1024
 EPSILON = 1e-06
 NEAR = 3
+PIECES = 2
 MESH = pl.DeviceIdType.MESH
 SCORE_SCALE = 1.0 / math.sqrt(HD)
 
@@ -147,24 +148,34 @@
 
     values, grads, keys, queries = range(4)
     hops = {}
+    size = rows // PIECES
     for which, ref, forward in (
         (values, vs, True), (grads, gs, False), (keys, ks, True), (queries, qs, False)
     ):
         peer = ahead[0] if forward else behind[0]
         for slot in range(1, reach + 1):
-            source = slot - 1
-            hops[which, slot] = remote(
-                ref.at[pl.ds(source * rows, rows)],
-                ref.at[pl.ds(slot * rows, rows)],
-                ring_send.at[which, slot - 1],
-                ring_recv.at[which, slot - 1],
-                peer,
-            )
-
-    def advance(which, step):
-        hops[which, step].wait_recv()
-        if step < reach:
-            hops[which, step + 1].start()
+            for piece in range(PIECES):
+                start = slot * rows + piece * size
+                number = (slot - 1) * PIECES + piece
+                hops[which, slot, piece] = remote(
+                    ref.at[pl.ds(start - rows, size)],
+                    ref.at[pl.ds(start, size)],
+                    ring_send.at[which, number],
+                    ring_recv.at[which, number],
+                    peer,
+                )
+
+    def launch(*chosen):
+        for piece in range(PIECES):
+            for which in chosen:
+                hops[which, 1, piece].start()
+
+    def advance(step, *chosen):
+        for piece in range(PIECES):
+            for which in chosen:
+                hops[which, step, piece].wait_recv()
+                if step < reach:
+                    hops[which, step + 1, piece].start()
 
     norm_copies = [
         remote(sums.at[head], sums.at[head], norm_send.at[t + 1], norm_recv.at[t + 1], peer)
@@ -172,8 +183,7 @@
     ]
     for copy in norm_copies:
         copy.start()
-    hops[values, 1].start()
-    hops[grads, 1].start()
+    launch(values, grads)
 
     for copy in norm_copies:
         copy.wait_recv()
@@ -195,8 +205,7 @@
     ]
     near_q, far_q = split_heads(q_normed, index)
     store_near(qs, near_q, rows)
-    hops[keys, 1].start()
-    hops[queries, 1].start()
+    launch(keys, queries)
     packed = jnp.concatenate(
         [part.reshape(classes, per_peer, HD) for part in (far_q, far_k, far_v, far_g)], axis=1
     )
@@ -223,8 +232,8 @@
             key_grads[h, block, :] = dot_nt(own_v, gs[block, cut])
 
     def ring_step(step):
-        for which in (values, grads, keys, queries):
-            advance(which, step)
+        advance(step, values, grads)
+        advance(step, keys, queries)
         products(step)
 
     products(0)
@@ -346,7 +355,7 @@
         ]
         + [pltpu.VMEM((classes, quad, HD), low)] * 4
         + [pltpu.VMEM((rows, near_width), wide)] * 3
-        + [dma((4, reach))] * 2
+        + [dma((4, reach * PIECES))] * 2
         + [dma((head_total,))] * 2
         + [dma((classes,))] * 4
         + [dma((reach + 1,))] * 2

time: 91 us -> 87.3 us (0.959)
  the two profiles are of different devices: /device:TPU:114 before, /device:TPU:118 now
where the time goes in v5:
time: 87.3 us; the launch traced here: 87.1 us
  Pallas kernels  83.3 us (95%)
  local copies, waits for them, and re-layouts  3.21 us (4%)
    pallas_call x1, Pallas kernels, on_device(): pl.pallas_call(functools.partial(backward_kernel, ctx_count, head_total),...  83.3 us
    unnamed x7, local copies, waits for them, and re-layouts  3.21 us

profile of v5, /device:TPU:118, one launch (start us, length us, event | category | flops | bytes accessed | tf_op | source)
XLA Modules:
  0.0 87.1 jit_solution(2123686364490763375)
XLA Ops:
  0.6 83.3 %backward.1 = (bf16[128,512]{1,0:T(8,128)(2,1)}, bf16[128,512]{1,0:T(8,128)(2,1)}, bf16[128,512]{1,0:T(8,128)(2,1)}) custom-call(s32[4]{0:T(128)} %kind_ref.1, bf16[128,512]{1,0:T(8,128)(2,1)} %q_ref.1, bf16[128,512]{1,0:T(8,128)(2,1)} %k_ref.1, bf16[128,512]{1,0:T(8,128)(2,1)} %v_ref.1, bf16[128,512]{1,0:T(8,128)(2,1)} %g_ref.1, f32[1,512]{1,0:T(1,128)} %bitcast.2, ...), custom_call_target="tpu_custom_call" | custom-call | tf_op jit(solution)/shard_map/backward/pallas_call | solution.py:345
  83.9 0.0 copy-start.1
  83.9 1.6 %copy.13 = bf16[128,512]{1,0:T(8,128)(2,1)} copy(bf16[128,512]{1,0:T(8,128)(2,1)} %get-tuple-element.6) | data formatting | bytes 262144
  85.5 0.0 copy-done.1
  85.5 0.0 copy-start
  85.5 0.7 copy.14
  86.2 0.3 copy-done
  86.5 0.7 copy.15
Async XLA Ops:
  83.9 1.6 %copy-start.1 = (bf16[128,512]{1,0:T(8,128)(2,1)S(1)}, bf16[128,512]{1,0:T(8,128)(2,1)}, u32[]{:S(2)}) copy-start(bf16[128,512]{1,0:T(8,128)(2,1)} %get-tuple-element.7) | copy-start | bytes 393220
  85.5 1.0 %copy-start = (bf16[128,512]{1,0:T(8,128)(2,1)S(1)}, bf16[128,512]{1,0:T(8,128)(2,1)}, u32[]{:S(2)}) copy-start(bf16[128,512]{1,0:T(8,128)(2,1)} %get-tuple-element.8) | copy-start | bytes 393220
